TPU v7x, 32 devices: a whole 2x2x4 slice. The times are simulated.
32 devices in a mesh: fsdp: 4 (over z), ctx: 4 (over x, core), tp: 2 (over y).
Axes of the slice: x: 2, y: 2, z: 4, core: 2. Of those that a mesh axis runs over, the one named last changes fastest.
Arguments:
- tokens: bfloat16 [4, 2176, 1536], P('fsdp', ('ctx', 'tp')), may hold values from -30 to 30
- segment_ids: int32 [4, 2176], P('fsdp', 'ctx'), may hold values from 0 to 7, never falling along the last dimension, each value on 1 to 1088 neighbouring positions
- wq: bfloat16 [1536, 1536], P('fsdp', 'tp'), may hold values from -0.15625 to 0.15625
- wk: bfloat16 [1536, 1536], P('fsdp', 'tp'), may hold values from -0.15625 to 0.15625
- wv: bfloat16 [1536, 1536], P('fsdp', 'tp'), may hold values from -0.15625 to 0.15625
- wo: bfloat16 [1536, 1536], P('tp', 'fsdp'), may hold values from -0.875 to 0.875
- w_gate: bfloat16 [1536, 4096], P('fsdp', 'tp'), may hold values from -0.15625 to 0.15625
- w_up: bfloat16 [1536, 4096], P('fsdp', 'tp'), may hold values from -0.15625 to 0.15625
- w_down: bfloat16 [4096, 1536], P('tp', 'fsdp'), may hold values from -0.09375 to 0.09375
- gain_attn: bfloat16 [1536], P('fsdp'), may hold values from 0.099609375 to 1.8984375
- gain_ffn: bfloat16 [1536], P('fsdp'), may hold values from 0.099609375 to 1.8984375
- cotangent: bfloat16 [4, 2176, 1536], P('fsdp', ('ctx', 'tp')), may hold values from -6 to 6
Outputs:
- layer_out: bfloat16 [4, 2176, 1536], P('fsdp', ('ctx', 'tp'))
- grad_input: float32 [4, 2176, 1536], P('fsdp', ('ctx', 'tp'))
- query_weight_gradient: float32 [1536, 1536], P('fsdp', 'tp')
- key_weight_gradient: float32 [1536, 1536], P('fsdp', 'tp')
- value_weight_gradient: float32 [1536, 1536], P('fsdp', 'tp')
- output_weight_gradient: float32 [1536, 1536], P('tp', 'fsdp')
- gate_weight_gradient: float32 [1536, 4096], P('fsdp', 'tp')
- up_weight_gradient: float32 [1536, 4096], P('fsdp', 'tp')
- down_weight_gradient: float32 [4096, 1536], P('tp', 'fsdp')
- grad_gain_attn: float32 [1536], P('fsdp')
- grad_gain_ffn: float32 [1536], P('fsdp')
Inputs may be any that keep to these rules, and one draw needn't show every extreme that they name: `segment_ids`: within each sequence the ids never fall; each document holds 1 to 1088 positions, and one document of every sequence holds exactly 1088.
All inputs are finite; a program needn't handle non-finite values.
Results may differ from a plain program's by a relative error of at most 0.024.
Values may be sent and summed in bfloat16 or wider, within the bound.
No kernel may reach another device: no remote copies, remote signals or barrier semaphores. Data moves between devices by JAX's collectives and lax.ppermute only.
A program may use at most 320 MiB of HBM per device.

v0:
```python
import jax
import jax.numpy as jnp
from jax import lax
from jax.sharding import PartitionSpec as P

HEAD_DIM = 64
EPSILON = 1e-05
MASKED = -1e30
BF16 = jnp.bfloat16
F32 = jnp.float32


def pull_fsdp(values, step):
    count = lax.axis_size("fsdp")
    return lax.ppermute(values, "fsdp", [(i, (i - step) % count) for i in range(count)])


def push_fsdp(values, step):
    count = lax.axis_size("fsdp")
    return lax.ppermute(values, "fsdp", [(i, (i + step) % count) for i in range(count)])


def swap_chip(values):
    return lax.ppermute(values, "ctx", [(i, i ^ 2) for i in range(lax.axis_size("ctx"))])


def swap_core(values):
    return lax.ppermute(values, "ctx", [(i, i ^ 1) for i in range(lax.axis_size("ctx"))])


def widen_rows(values):
    if lax.axis_size("tp") != 2:
        return lax.all_gather(values, "tp", axis=0, tiled=True)
    other = lax.ppermute(values, "tp", [(0, 1), (1, 0)])
    first = lax.axis_index("tp") == 0
    return jnp.concatenate(
        [jnp.where(first, values, other), jnp.where(first, other, values)], axis=0
    )


def narrow_rows(values):
    count = lax.axis_size("tp")
    if count != 2:
        return lax.psum_scatter(values.astype(BF16), "tp", scatter_dimension=0, tiled=True).astype(
            F32
        )
    rows = values.shape[0] // count
    me = lax.axis_index("tp")
    sent = lax.dynamic_slice_in_dim(values, (1 - me) * rows, rows, 0).astype(BF16)
    kept = lax.dynamic_slice_in_dim(values, me * rows, rows, 0)
    return kept + lax.ppermute(sent, "tp", [(0, 1), (1, 0)]).astype(F32)


def roll_columns(values, blocks):
    width = values.shape[-1]
    block = width // lax.axis_size("fsdp")
    twice = jnp.concatenate([values, values], axis=-1)
    return lax.dynamic_slice_in_dim(twice, blocks * block, width, values.ndim - 1)


def to_relative(values):
    return roll_columns(values, lax.axis_index("fsdp"))


def to_natural(values):
    count = lax.axis_size("fsdp")
    return roll_columns(values, (count - lax.axis_index("fsdp")) % count)


def after(values, earlier):
    return lax.optimization_barrier((values, earlier))[0]


def quarter(values, index, axis):
    size = values.shape[axis] // 4
    return lax.dynamic_slice_in_dim(values, index * size, size, axis)


def gather_quarters(shard, fsdp_axis, quarter_axis, earlier=None):
    count = lax.axis_size("fsdp")
    place = lax.axis_index("ctx")
    own = quarter(shard, place, quarter_axis)
    if earlier is not None:
        own = after(own, earlier)
    parts = [pull_fsdp(own, step) for step in range(1, count)]
    mine = jnp.concatenate([own] + parts, axis=fsdp_axis)
    crossed = swap_chip(jnp.concatenate(parts, axis=fsdp_axis))
    across = jnp.concatenate([quarter(shard, place ^ 2, quarter_axis), crossed], axis=fsdp_axis)
    return ([mine, swap_core(mine), across, swap_core(across)], parts[-1])


def gather_plain(shard, fsdp_axis, earlier=None):
    count = lax.axis_size("fsdp")
    if earlier is not None:
        shard = after(shard, earlier)
    parts = [pull_fsdp(shard, step) for step in range(1, count)]
    return (jnp.concatenate([shard] + parts, axis=fsdp_axis), parts[-1])


def add_halves(left, right):
    return (left.astype(F32) + right.astype(F32)).astype(BF16)


def fsdp_total(values, fsdp_axis):
    count = lax.axis_size("fsdp")
    pieces = jnp.split(values, count, axis=fsdp_axis)
    total = pieces[0].astype(F32)
    for step in range(1, count):
        total = total + push_fsdp(pieces[step], step).astype(F32)
    return total


def reduce_quarters(blocks, fsdp_axis, quarter_axis):
    place = lax.axis_index("ctx")
    came = swap_core(jnp.stack([blocks[1], blocks[3]]))
    near = add_halves(blocks[0], came[0])
    far = add_halves(blocks[2], came[1])
    mine = add_halves(near, swap_chip(far))
    own = fsdp_total(mine, fsdp_axis).astype(BF16)
    crossed = swap_chip(own)
    core_own, core_crossed = (swap_core(own), swap_core(crossed))
    odd_core, odd_chip = (place % 2 == 1, place >= 2)
    pick = jnp.where
    a0, a1 = (pick(odd_core, core_own, own), pick(odd_core, own, core_own))
    b0, b1 = (pick(odd_core, core_crossed, crossed), pick(odd_core, crossed, core_crossed))
    order = [
        pick(odd_chip, b0, a0),
        pick(odd_chip, b1, a1),
        pick(odd_chip, a0, b0),
        pick(odd_chip, a1, b1),
    ]
    return jnp.concatenate(order, axis=quarter_axis).astype(F32)


def reduce_plain(grad, fsdp_axis):
    return lax.psum(fsdp_total(grad, fsdp_axis).astype(BF16), "ctx").astype(F32)


def fetch_window(rows):
    count = lax.axis_size("ctx")
    even = lax.axis_index("ctx") % 2 == 0
    own = widen_rows(rows)
    far = widen_rows(lax.ppermute(rows, "ctx", [(i, i + 2) for i in range(count - 2)]))
    near = swap_core(jnp.where(even, own, far))
    return jnp.concatenate([far, near, own], axis=0)


def return_window(far, near, own):
    count = lax.axis_size("ctx")
    even = lax.axis_index("ctx") % 2 == 0
    came = swap_core(near.astype(BF16)).astype(F32)
    own = narrow_rows(own + jnp.where(even, came, 0.0))
    far = narrow_rows(far + jnp.where(even, 0.0, came)).astype(BF16)
    return own + lax.ppermute(far, "ctx", [(i, i - 2) for i in range(2, count)]).astype(F32)


def fetch_ids(ids):
    count = lax.axis_size("ctx")
    even = lax.axis_index("ctx") % 2 == 0
    far = lax.ppermute(ids, "ctx", [(i, i + 2) for i in range(count - 2)])
    return jnp.concatenate([far, swap_core(jnp.where(even, ids, far)), ids])


def rope_tables(offset, row_count, half_dim):
    where_at = (offset + jnp.arange(row_count, dtype=jnp.int32)).astype(F32)
    inv_freq = 10000.0 ** (-jnp.arange(half_dim, dtype=F32) * 2.0 / (2 * half_dim))
    angles = where_at[:, None] * inv_freq[None, :]
    return (jnp.cos(angles), jnp.sin(angles))


def rotate(values, cos_rows, sin_rows, direction):
    half_dim = values.shape[-1] // 2
    first_half = values[..., :half_dim]
    second_half = values[..., half_dim:]
    cos_part = cos_rows[:, None, :]
    sin_part = sin_rows[:, None, :] * direction
    return jnp.concatenate(
        [
            first_half * cos_part - second_half * sin_part,
            second_half * cos_part + first_half * sin_part,
        ],
        axis=-1,
    )


def normalize_back(values, inverse, gain, grad_rows):
    scaled = grad_rows * gain
    return inverse * scaled - values * inverse**3 * jnp.mean(
        scaled * values, axis=-1, keepdims=True
    )


def dot(left, right):
    return jnp.dot(left, right, preferred_element_type=F32)


def dot_nt(left, right):
    return lax.dot_general(left, right, (((1,), (1,)), ((), ())), preferred_element_type=F32)


def dot_tn(left, right):
    return lax.dot_general(left, right, (((0,), (0,)), ((), ())), preferred_element_type=F32)


def shards(
    tokens, segment_ids, wq, wk, wv, wo, w_gate, w_up, w_down, gain_attn, gain_ffn, cotangent
):
    tokens, cotangent, segment_ids = (tokens[0], cotangent[0], segment_ids[0])
    ctx_rows = segment_ids.shape[0]
    head_count = wq.shape[1] // HEAD_DIM
    row_width = wq.shape[1]
    scale = HEAD_DIM ** (-0.5)
    by_heads = head_count % 4 == 0
    first_query = lax.axis_index("ctx") * ctx_rows
    cos_rows, sin_rows = rope_tables(first_query - 2 * ctx_rows, 3 * ctx_rows, HEAD_DIM // 2)
    qkv = jnp.stack([wq, wk, wv])
    if by_heads:
        qkv_parts, mark = gather_quarters(qkv, 1, 2)
        qkv_whole = jnp.concatenate(qkv_parts, axis=2)
        out_parts, mark = gather_quarters(wo, 1, 0, mark)
        out_whole = jnp.concatenate(out_parts, axis=0)
    else:
        qkv_whole, mark = gather_plain(qkv, 1)
        out_whole, mark = gather_plain(wo, 1, mark)
    wide_parts, mark = gather_quarters(jnp.stack([w_gate, w_up]), 1, 2, mark)
    wide_whole = jnp.concatenate(wide_parts, axis=2)
    gate_whole, up_whole = (wide_whole[0], wide_whole[1])
    down_parts, mark = gather_quarters(w_down, 1, 0, mark)
    down_whole = jnp.concatenate(down_parts, axis=0)
    gains, _ = gather_plain(jnp.stack([gain_attn, gain_ffn]), 1)
    gain_one, gain_two = (gains[0].astype(F32), gains[1].astype(F32))
    inputs = to_relative(tokens).astype(F32)
    dy_rows = to_relative(cotangent)
    inv_one = lax.rsqrt(jnp.mean(inputs * inputs, axis=-1, keepdims=True) + EPSILON)
    normed_window = fetch_window((inputs * inv_one * gain_one).astype(BF16))
    normed = normed_window[2 * ctx_rows :]
    dy_wide = widen_rows(dy_rows)

    def heads(values):
        return values.reshape(values.shape[0], head_count, HEAD_DIM)

    cos_own, sin_own = (cos_rows[2 * ctx_rows :], sin_rows[2 * ctx_rows :])
    queries = rotate(heads(dot(normed, qkv_whole[0])), cos_own, sin_own, 1.0).astype(BF16)
    keys = rotate(heads(dot(normed_window, qkv_whole[1])), cos_rows, sin_rows, 1.0).astype(BF16)
    values = heads(dot(normed_window, qkv_whole[2]).astype(BF16))
    segment_window = fetch_ids(segment_ids)
    pos_query = first_query + jnp.arange(ctx_rows, dtype=jnp.int32)
    pos_key = first_query - 2 * ctx_rows + jnp.arange(3 * ctx_rows, dtype=jnp.int32)
    allowed = (
        (segment_ids[:, None] == segment_window[None, :])
        & (pos_key[None, :] <= pos_query[:, None])
        & (pos_key[None, :] >= 0)
    )[None]
    scores = jnp.einsum("qhd,khd->hqk", queries, keys, preferred_element_type=F32) * scale
    scores = jnp.where(allowed, scores, MASKED)
    top = jnp.max(scores, axis=-1, keepdims=True)
    powers = jnp.where(allowed, jnp.exp(scores - top), 0.0)
    sums = jnp.sum(powers, axis=-1, keepdims=True)
    weighted = jnp.einsum("hqk,khd->hqd", powers.astype(BF16), values, preferred_element_type=F32)
    attended = jnp.transpose(weighted / sums, (1, 0, 2))
    log_sums = top + jnp.log(sums)
    attended_low = attended.astype(BF16).reshape(ctx_rows, row_width)
    residual = inputs + narrow_rows(dot(attended_low, out_whole))
    inv_two = lax.rsqrt(jnp.mean(residual * residual, axis=-1, keepdims=True) + EPSILON)
    normed_two = widen_rows((residual * inv_two * gain_two).astype(BF16))
    gate = dot(normed_two, gate_whole)
    up = dot(normed_two, up_whole)
    sig = jax.nn.sigmoid(gate)
    silu = gate * sig
    hidden = (silu * up).astype(BF16)
    hidden_grad = dot_nt(dy_wide, down_whole)
    gate_grad = (hidden_grad * up * sig * (1.0 + gate * (1.0 - sig))).astype(BF16)
    up_grad = (hidden_grad * silu).astype(BF16)
    normed_two_grad = narrow_rows(dot_nt(gate_grad, gate_whole) + dot_nt(up_grad, up_whole))
    layer_out = residual + narrow_rows(dot(hidden, down_whole))
    down_grad = dot_tn(hidden, dy_wide).astype(BF16)
    wide_grad = jnp.stack(
        [dot_tn(normed_two, gate_grad).astype(BF16), dot_tn(normed_two, up_grad).astype(BF16)]
    )
    down_total = reduce_quarters(jnp.split(down_grad, 4, axis=0), 1, 0)
    wide_total = reduce_quarters(jnp.split(wide_grad, 4, axis=2), 1, 2)
    gain_two_grad = jnp.sum(normed_two_grad * residual * inv_two, axis=0)
    resid_grad = dy_rows.astype(F32) + normalize_back(residual, inv_two, gain_two, normed_two_grad)
    attention_grad = widen_rows(resid_grad.astype(BF16))
    out_weight_grad = dot_tn(attended_low, attention_grad).astype(BF16)
    out_grad = heads(dot_nt(attention_grad, out_whole).astype(BF16))
    delta = jnp.sum(out_grad.astype(F32) * attended, axis=-1)
    soft = jnp.where(allowed, jnp.exp(scores - log_sums), 0.0)
    prob_grad = jnp.einsum("qhd,khd->hqk", out_grad, values, preferred_element_type=F32)
    score_grad = (soft * (prob_grad - jnp.transpose(delta)[:, :, None])).astype(BF16)
    query_grad = jnp.einsum("hqk,khd->qhd", score_grad, keys, preferred_element_type=F32) * scale
    key_add = jnp.einsum("hqk,qhd->khd", score_grad, queries, preferred_element_type=F32) * scale
    value_add = jnp.einsum("hqk,qhd->khd", soft.astype(BF16), out_grad, preferred_element_type=F32)
    query_low = rotate(query_grad, cos_own, sin_own, -1.0).astype(BF16).reshape(ctx_rows, row_width)
    key_low = (
        rotate(key_add, cos_rows, sin_rows, -1.0).astype(BF16).reshape(3 * ctx_rows, row_width)
    )
    value_low = value_add.astype(BF16).reshape(3 * ctx_rows, row_width)
    qkv_grad = jnp.stack(
        [
            dot_tn(normed, query_low).astype(BF16),
            dot_tn(normed_window, key_low).astype(BF16),
            dot_tn(normed_window, value_low).astype(BF16),
        ]
    )
    if by_heads:
        out_total = reduce_quarters(jnp.split(out_weight_grad, 4, axis=0), 1, 0)
        qkv_total = reduce_quarters(jnp.split(qkv_grad, 4, axis=2), 1, 2)
    else:
        out_total = reduce_plain(out_weight_grad, 1)
        qkv_total = reduce_plain(qkv_grad, 1)
    normed_parts = dot_nt(key_low, qkv_whole[1]) + dot_nt(value_low, qkv_whole[2])
    far, near, own = (normed_parts[i * ctx_rows : (i + 1) * ctx_rows] for i in range(3))
    normed_grad = return_window(far, near, own + dot_nt(query_low, qkv_whole[0]))
    gain_one_grad = jnp.sum(normed_grad * inputs * inv_one, axis=0)
    grad_input = resid_grad + normalize_back(inputs, inv_one, gain_one, normed_grad)
    gain_grads = lax.psum(
        to_natural(jnp.stack([gain_one_grad, gain_two_grad])), ("fsdp", "ctx", "tp")
    )
    gain_rows = gain_attn.shape[0]
    gain_own = lax.dynamic_slice_in_dim(
        gain_grads, lax.axis_index("fsdp") * gain_rows, gain_rows, 1
    )
    return (
        to_natural(layer_out.astype(BF16))[None],
        to_natural(grad_input)[None],
        qkv_total[0],
        qkv_total[1],
        qkv_total[2],
        out_total,
        wide_total[0],
        wide_total[1],
        down_total,
        gain_own[0],
        gain_own[1],
    )


def solution(mesh):
    rows = P("fsdp", ("ctx", "tp"), None)
    into, outof, gain = (P("fsdp", "tp"), P("tp", "fsdp"), P("fsdp"))
    return jax.shard_map(
        shards,
        mesh=mesh,
        in_specs=(
            rows,
            P("fsdp", "ctx"),
            into,
            into,
            into,
            outof,
            into,
            into,
            outof,
            gain,
            gain,
            rows,
        ),
        out_specs=(rows, rows, into, into, into, outof, into, into, outof, gain, gain),
        check_vma=False,
    )
```

profile of v0, /device:TPU:1, one launch (start us, length us, event | category | flops | bytes accessed | tf_op | source)
XLA Modules:
  0.0 983.1 jit_solution(6870542707094857288)
XLA Ops:
  45.6 9.8 collective-permute-start.15
  58.1 4.9 collective-permute-done.15
  63.0 19.4 %collective-permute-start.24 = (bf16[2,384,512]{2,1,0:T(8,128)(2,1)S(1)}, bf16[2,384,512]{2,1,0:T(8,128)(2,1)S(1)}, u32[]{:S(2)}, u32[]{:S(2)}) collective-permute-start(bf16[2,384,512]{2,1,0:T(8,128)(2,1)S(1)} %copy-done.34), channel_id=1, source_target_pairs={{0,16},{8,24},{16,0},{24,8},{1,17},{9,25},{17,1},{25,9},{2,18},{10... | collective-permute-start | bytes 2359304 | tf_op jit(solution)/shard_map/ppermute | solution.py:15
  92.5 6.0 collective-permute-done.19
  101.8 13.3 %collective-permute-done.23 = bf16[2,384,512]{2,1,0:T(8,128)(2,1)S(1)} collective-permute-done((bf16[2,384,512]{2,1,0:T(8,128)(2,1)S(1)}, bf16[2,384,512]{2,1,0:T(8,128)(2,1)S(1)}, u32[]{:S(2)}, u32[]{:S(2)}) %collective-permute-start.23) | collective-permute-done | bytes 786464 | tf_op jit(solution)/shard_map/ppermute | solution.py:15
  115.1 25.5 %collective-permute-start.31 = (bf16[512,384]{1,0:T(8,128)(2,1)S(1)}, bf16[512,384]{1,0:T(8,128)(2,1)S(1)}, u32[]{:S(2)}, u32[]{:S(2)}) collective-permute-start(bf16[512,384]{1,0:T(8,128)(2,1)S(1)} %copy-done.46), channel_id=1, source_target_pairs={{0,8},{8,16},{16,24},{24,0},{1,9},{9,17},{17,25},{25,1},{2,10},{10... | collective-permute-start | bytes 1179656 | tf_op jit(solution)/shard_map/ppermute | solution.py:15
  147.1 6.1 collective-permute-start.9
  153.2 8.4 collective-permute-done.30
  171.5 15.6 %collective-permute-done.33 = bf16[512,1152]{1,0:T(8,128)(2,1)S(1)} collective-permute-done((bf16[512,1152]{1,0:T(8,128)(2,1)S(1)}, bf16[512,1152]{1,0:T(8,128)(2,1)S(1)}, u32[]{:S(2)}, u32[]{:S(2)}) %collective-permute-start.33) | collective-permute-done | bytes 1179680 | tf_op jit(solution)/shard_map/ppermute | solution.py:24
  195.5 11.4 %pad_maximum_fusion.1 = bf16[3,1536,768]{1,2,0:T(8,128)(2,1)S(1)} fusion(bf16[3,1536,192]{1,2,0:T(8,128)(2,1)S(1)} %collective-permute-done.11, bf16[3,1152,192]{1,2,0:T(8,128)(2,1)S(1)} %collective-permute-done.10, bf16[3,384,192]{1,2,0:T(8,128)(2,1)S(1)} %copy-done.22, bf16[3,1536,192]{1,2,0:T(8,128)(2,1)S(1)} %collective-permute-done.9, ...), kind=kLoop, calls=%fused_computation.23 | loop fusion | flops 56623104 | bytes 14155776 | tf_op jit(solution)/shard_map/concatenate | solution.py:219
  212.2 5.3 convolution_convert_fusion.7
  221.9 7.7 fusion.18
  233.0 20.2 %fusion.3 = (f32[12,544]{1,0:T(8,128)S(1)}, f32[12,544,1632]{2,1,0:T(8,128)}) fusion(pred[544,1632]{1,0:T(8,128)(4,1)} %and_and_fusion, bf16[1632,12,32]{0,2,1:T(8,128)(2,1)} %get-tuple-element.85, bf16[1632,12,32]{0,2,1:T(8,128)(2,1)} %get-tuple-element.84, bf16[544,12,32]{0,2,1:T(8,128)(2,1)} %get-tuple-element.103, ...), kind=kOutput, calls=%fused_computation.7 | convolution fusion | flops 1402312320 | bytes 46871040 | tf_op jit(solution)/shard_map/qhd,khd->hqk/dot_general | solution.py:254
  253.2 23.3 %fusion = f32[12,544]{1,0:T(8,128)S(1)} fusion(f32[12,544,1632]{2,1,0:T(8,128)} %get-tuple-element.150, f32[12,544]{1,0:T(8,128)S(1)} %get-tuple-element.149, pred[544,1632]{1,0:T(8,128)(4,1)} %and_and_fusion), kind=kLoop, calls=%fused_computation.4 | loop fusion | flops 53261952 | bytes 43554816 | tf_op jit(solution)/shard_map/reduce_sum | solution.py:258
  276.5 20.9 %fusion.66 = (bf16[544,12,64]{0,2,1:T(8,128)(2,1)}, f32[12,544,64]{1,2,0:T(8,128)}) fusion(f32[544,12]{0,1:T(8,128)S(1)} %bitcast.196, bf16[1632,12,64]{0,2,1:T(8,128)(2,1)} %bitcast.182, f32[12,544,1632]{2,1,0:T(8,128)} %get-tuple-element.150, f32[12,544]{1,0:T(8,128)S(1)} %get-tuple-element.149, pred[544,1632]{1,0:T(8,128)(4,1)} %and_and_fusion), kind=kOutput, calls=%fused_computation.216 | convolution fusion | flops 1417777152 | bytes 48568320 | tf_op jit(solution)/shard_map/hqk,khd->hqd/dot_general | solution.py:259
  305.8 15.9 %collective-permute-done.21 = bf16[272,1536]{1,0:T(8,128)(2,1)S(1)} collective-permute-done((bf16[272,1536]{1,0:T(8,128)(2,1)S(1)}, bf16[272,1536]{1,0:T(8,128)(2,1)S(1)}, u32[]{:S(2)}, u32[]{:S(2)}) %collective-permute-start.21) | collective-permute-done | bytes 835616 | tf_op jit(solution)/shard_map/ppermute | solution.py:51
  323.5 11.3 %fusion.59 = f32[544,2048]{1,0:T(8,128)} fusion(bf16[272,1536]{1,0:T(8,128)(2,1)S(1)} %get-tuple-element.117, bf16[272,1536]{1,0:T(8,128)(2,1)S(1)} %get-tuple-element.116, bf16[512,1536]{1,0:T(8,128)(2,1)} %collective-permute-done.34, bf16[512,1152]{1,0:T(8,128)(2,1)S(1)} %copy-done.51, bf16[512,384]{1,0:T(8,128)(2,1)S(1)} %copy-done.45, ...), kind=kOutput, calls=%fused_computation.184 | convolution fusion | flops 3457351680 | bytes 12419072 | tf_op jit(solution)/shard_map/dot_general | solution.py:198
  334.8 6.6 collective-permute-done.22
  341.9 28.1 %pad_maximum_fusion = bf16[2,1536,2048]{2,1,0:T(8,128)(2,1)S(1)} fusion(bf16[2,1536,512]{2,1,0:T(8,128)(2,1)S(1)} %collective-permute-done.28, bf16[2,1152,512]{2,1,0:T(8,128)(2,1)S(1)} %copy-done.7, bf16[2,384,512]{2,1,0:T(8,128)(2,1)S(1)} %copy-done.15, bf16[2,1536,512]{2,1,0:T(8,128)(2,1)} %collective-permute-done.26, ...), kind=kLoop, calls=%fused_computation.18 | loop fusion | flops 62914560 | bytes 25165824 | tf_op jit(solution)/shard_map/concatenate | solution.py:226
  370.0 5.8 fusion.17
  375.8 9.4 multiply_convert_fusion.2
  385.2 5.4 fusion.16
  390.7 5.4 fusion.11
  396.1 7.1 convolution_convert_fusion
  403.2 6.4 fusion.93
  411.4 7.2 fusion.10
  418.6 9.8 %fusion.28 = f32[544,1536]{1,0:T(8,128)} fusion(f32[544,1536]{1,0:T(8,128)} %fusion.16, bf16[544,2048]{1,0:T(8,128)(2,1)} %get-tuple-element.71, bf16[2,1536,2048]{2,1,0:T(8,128)(2,1)S(1)} %pad_maximum_fusion), kind=kOutput, calls=%fused_computation.80 | convolution fusion | flops 3423387648 | bytes 15204352 | tf_op jit(solution)/shard_map/dot_general | solution.py:198
  437.5 10.7 %collective-permute-done.37 = bf16[272,1536]{1,0:T(8,128)(2,1)S(1)} collective-permute-done((bf16[272,1536]{1,0:T(8,128)(2,1)S(1)}, bf16[272,1536]{1,0:T(8,128)(2,1)S(1)}, u32[]{:S(2)}, u32[]{:S(2)}) %collective-permute-start.37) | collective-permute-done | bytes 835616 | tf_op jit(solution)/shard_map/ppermute | solution.py:51
  461.1 7.5 collective-permute-done.38
  478.1 19.7 %fusion.23 = bf16[12,64,1632]{2,1,0:T(8,128)(2,1)} fusion(bf16[544,12,64]{0,2,1:T(8,128)(2,1)S(1)} %bitcast.180, f32[12,544,1632]{2,1,0:T(8,128)} %get-tuple-element.150, f32[12,544]{1,0:T(8,128)S(1)} %log_add_fusion, pred[544,1632]{1,0:T(8,128)(4,1)S(1)} %copy-done.32), kind=kOutput, calls=%fused_computation.70 | convolution fusion | flops 1418194944 | bytes 46871040 | tf_op jit(solution)/shard_map/hqk,qhd->khd/dot_general | solution.py:293
  497.9 27.7 %multiply_convert_fusion = bf16[12,544,1632]{2,1,0:T(8,128)(2,1)} fusion(f32[12,544,1632]{2,1,0:T(8,128)} %get-tuple-element.150, bf16[544,12,64]{0,2,1:T(8,128)(2,1)} %bitcast.181, bf16[1632,12,64]{0,2,1:T(8,128)(2,1)} %bitcast.183, f32[12,544]{1,0:T(8,128)S(1)} %bitcast.200, f32[12,544]{1,0:T(8,128)S(1)} %log_add_fusion, pred[544,1632]{1,0:T(8,128)(4,1)} %and_and_fusion), kind=kOutput, calls=%fused_computation | convolution fusion | flops 1438248960 | bytes 68204544 | tf_op jit(solution)/shard_map/qhd,khd->hqk/dot_general | solution.py:289
  525.6 10.9 %multiply_bitcast_fusion.1 = f32[544,12,64]{0,2,1:T(8,128)S(1)} fusion(bf16[12,544,1632]{2,1,0:T(8,128)(2,1)} %multiply_convert_fusion, bf16[1632,12,32]{0,2,1:T(8,128)(2,1)S(1)} %copy-done.20, bf16[1632,12,32]{0,2,1:T(8,128)(2,1)S(1)} %copy-done.19), kind=kOutput, calls=%fused_computation.115 | convolution fusion | flops 1369104384 | bytes 25485312 | tf_op jit(solution)/shard_map/hqk,khd->qhd/dot_general | solution.py:291
  536.5 10.4 %multiply_bitcast_fusion = f32[1632,12,64]{0,2,1:T(8,128)S(1)} fusion(bf16[12,544,1632]{2,1,0:T(8,128)(2,1)} %multiply_convert_fusion, bf16[544,12,32]{0,2,1:T(8,128)(2,1)} %get-tuple-element.103, bf16[544,12,32]{0,2,1:T(8,128)(2,1)} %get-tuple-element.102), kind=kOutput, calls=%fused_computation.41 | convolution fusion | flops 1366597632 | bytes 27156480 | tf_op jit(solution)/shard_map/hqk,qhd->khd/dot_general | solution.py:292
  559.2 6.8 fusion.41
  565.9 9.2 convolution_add_fusion
  580.9 4.8 fusion.37
  596.9 7.6 collective-permute-done.52
  605.9 12.1 %collective-permute-start.53 = (bf16[192,384]{1,0:T(8,128)(2,1)S(1)}, bf16[192,384]{1,0:T(8,128)(2,1)S(1)}, u32[]{:S(2)}, u32[]{:S(2)}) collective-permute-start(bf16[192,384]{1,0:T(8,128)(2,1)S(1)} %get-tuple-element.135), channel_id=1, source_target_pairs={{0,8},{8,16},{16,24},{24,0},{1,9},{9,17},{17,25},{25,1},{2,10},{10... | collective-permute-start | bytes 442376 | tf_op jit(solution)/shard_map/ppermute | solution.py:20
  625.2 9.4 collective-permute-done.54
  635.6 6.3 fusion.26
  657.9 22.2 %collective-permute-done.68 = bf16[512,1536]{1,0:T(8,128)(2,1)S(1)} collective-permute-done((bf16[512,1536]{1,0:T(8,128)(2,1)S(1)}, bf16[512,1536]{1,0:T(8,128)(2,1)S(1)}, u32[]{:S(2)}, u32[]{:S(2)}) %collective-permute-start.68) | collective-permute-done | bytes 1572896 | tf_op jit(solution)/shard_map/ppermute | solution.py:24
  686.8 11.2 %collective-permute-done.42 = bf16[272,1536]{1,0:T(8,128)(2,1)S(1)} collective-permute-done((bf16[272,1536]{1,0:T(8,128)(2,1)S(1)}, bf16[272,1536]{1,0:T(8,128)(2,1)S(1)}, u32[]{:S(2)}, u32[]{:S(2)}) %collective-permute-start.42) | collective-permute-done | bytes 835616 | tf_op jit(solution)/shard_map/ppermute | solution.py:154
  699.1 135.8 %psum.7 = f32[2,1536]{1,0:T(2,128)S(1)} all-reduce(f32[2,1536]{1,0:T(2,128)S(1)} %fusion.68), channel_id=1, replica_groups=mesh['fsdp'=4,'ctx'=4,'tp'=2] {'fsdp','ctx','tp'}, use_global_device_ids=true, to_apply=%region_9.10 | all-reduce | flops 3072 | bytes 24576 | tf_op jit(solution)/shard_map/psum | solution.py:317
  854.7 7.7 collective-permute-done.47
  862.4 15.3 %collective-permute-start.74 = (bf16[512,384]{1,0:T(8,128)(2,1)S(1)}, bf16[512,384]{1,0:T(8,128)(2,1)S(1)}, u32[]{:S(2)}, u32[]{:S(2)}) collective-permute-start(bf16[512,384]{1,0:T(8,128)(2,1)S(1)} %add_convert_fusion.10), channel_id=1, source_target_pairs={{0,2},{2,0},{4,6},{6,4},{1,3},{3,1},{5,7},{7,5},{8,10},{10,8},{12,... | collective-permute-start | bytes 1179656 | tf_op jit(solution)/shard_map/ppermute | solution.py:28
  877.7 22.1 %collective-permute-done.46 = bf16[3,384,192]{1,2,0:T(8,128)(2,1)S(1)} collective-permute-done((bf16[3,384,192]{1,2,0:T(8,128)(2,1)S(1)}, bf16[3,384,192]{1,2,0:T(8,128)(2,1)S(1)}, u32[]{:S(2)}, u32[]{:S(2)}) %collective-permute-start.46) | collective-permute-done | bytes 442400 | tf_op jit(solution)/shard_map/ppermute | solution.py:20
  905.6 44.8 %collective-permute-done.62 = bf16[2,384,512]{2,1,0:T(8,128)(2,1)S(1)} collective-permute-done((bf16[2,384,512]{2,1,0:T(8,128)(2,1)S(1)}, bf16[2,384,512]{2,1,0:T(8,128)(2,1)S(1)}, u32[]{:S(2)}, u32[]{:S(2)}) %collective-permute-start.62) | collective-permute-done | bytes 786464 | tf_op jit(solution)/shard_map/ppermute | solution.py:20
  957.7 11.7 %collective-permute-done.64 = bf16[2,384,512]{2,1,0:T(8,128)(2,1)} collective-permute-done((bf16[2,384,512]{2,1,0:T(8,128)(2,1)}, bf16[2,384,512]{2,1,0:T(8,128)(2,1)}, u32[]{:S(2)}, u32[]{:S(2)}) %collective-permute-start.64) | collective-permute-done | bytes 786464 | tf_op jit(solution)/shard_map/ppermute | solution.py:24
  (462 shorter events, 250.7 us)
Async XLA Ops:
  2.0 22.9 %collective-permute-start.4 = (bf16[2,384]{1,0:T(2,128)(2,1)S(1)}, bf16[2,384]{1,0:T(2,128)(2,1)S(1)}, u32[]{:S(2)}, u32[]{:S(2)}) collective-permute-start(bf16[2,384]{1,0:T(2,128)(2,1)S(1)} %pad_maximum_fusion.39), channel_id=1, source_target_pairs={{0,8},{8,16},{16,24},{24,0},{1,9},{9,17},{17,25},{25,1},{2,10},{10... | collective-permute-start | bytes 4616 | tf_op jit(solution)/shard_map/ppermute | solution.py:15
  4.2 23.7 %collective-permute-start.3 = (bf16[2,384]{1,0:T(2,128)(2,1)S(1)}, bf16[2,384]{1,0:T(2,128)(2,1)S(1)}, u32[]{:S(2)}, u32[]{:S(2)}) collective-permute-start(bf16[2,384]{1,0:T(2,128)(2,1)S(1)} %pad_maximum_fusion.39), channel_id=1, source_target_pairs={{0,16},{8,24},{16,0},{24,8},{1,17},{9,25},{17,1},{25,9},{2,18},{10... | collective-permute-start | bytes 4616 | tf_op jit(solution)/shard_map/ppermute | solution.py:15
  6.5 24.5 %collective-permute-start.2 = (bf16[2,384]{1,0:T(2,128)(2,1)S(1)}, bf16[2,384]{1,0:T(2,128)(2,1)S(1)}, u32[]{:S(2)}, u32[]{:S(2)}) collective-permute-start(bf16[2,384]{1,0:T(2,128)(2,1)S(1)} %pad_maximum_fusion.39), channel_id=1, source_target_pairs={{0,24},{8,0},{16,8},{24,16},{1,25},{9,1},{17,9},{25,17},{2,26},{10... | collective-permute-start | bytes 4616 | tf_op jit(solution)/shard_map/ppermute | solution.py:15
  12.1 31.7 %collective-permute-start.8 = (bf16[3,384,192]{1,2,0:T(8,128)(2,1)S(1)}, bf16[3,384,192]{1,2,0:T(8,128)(2,1)S(1)}, u32[]{:S(2)}, u32[]{:S(2)}) collective-permute-start(bf16[3,384,192]{1,2,0:T(8,128)(2,1)S(1)} %get-tuple-element.112), channel_id=1, source_target_pairs={{0,8},{8,16},{16,24},{24,0},{1,9},{9,17},{17,25},{25,1},{2,10},{10... | collective-permute-start | bytes 1327112 | tf_op jit(solution)/shard_map/ppermute | solution.py:15
  12.5 31.5 %collective-permute-start.7 = (bf16[3,384,192]{1,2,0:T(8,128)(2,1)S(1)}, bf16[3,384,192]{1,2,0:T(8,128)(2,1)S(1)}, u32[]{:S(2)}, u32[]{:S(2)}) collective-permute-start(bf16[3,384,192]{1,2,0:T(8,128)(2,1)S(1)} %get-tuple-element.112), channel_id=1, source_target_pairs={{0,16},{8,24},{16,0},{24,8},{1,17},{9,25},{17,1},{25,9},{2,18},{10... | collective-permute-start | bytes 1327112 | tf_op jit(solution)/shard_map/ppermute | solution.py:15
  24.9 20.7 %collective-permute-start.6 = (bf16[3,384,192]{1,2,0:T(8,128)(2,1)S(1)}, bf16[3,384,192]{1,2,0:T(8,128)(2,1)S(1)}, u32[]{:S(2)}, u32[]{:S(2)}) collective-permute-start(bf16[3,384,192]{1,2,0:T(8,128)(2,1)S(1)} %get-tuple-element.112), channel_id=1, source_target_pairs={{0,24},{8,0},{16,8},{24,16},{1,25},{9,1},{17,9},{25,17},{2,26},{10... | collective-permute-start | bytes 1327112 | tf_op jit(solution)/shard_map/ppermute | solution.py:15
  35.8 52.6 %collective-permute-start.12 = (bf16[272,1536]{1,0:T(8,128)(2,1)}, bf16[272,1536]{1,0:T(8,128)(2,1)}, u32[]{:S(2)}, u32[]{:S(2)}) collective-permute-start(bf16[272,1536]{1,0:T(8,128)(2,1)} %fusion.46), channel_id=1, source_target_pairs={{0,4},{2,6},{1,5},{3,7},{8,12},{10,14},{9,13},{11,15},{16,20},{18,... | collective-permute-start | bytes 2506760 | tf_op jit(solution)/shard_map/ppermute | solution.py:143
  40.6 49.1 %collective-permute-start.5 = (bf16[272,1536]{1,0:T(8,128)(2,1)}, bf16[272,1536]{1,0:T(8,128)(2,1)}, u32[]{:S(2)}, u32[]{:S(2)}) collective-permute-start(bf16[272,1536]{1,0:T(8,128)(2,1)} %fusion.46), channel_id=1, source_target_pairs={{0,1},{1,0},{2,3},{3,2},{4,5},{5,4},{6,7},{7,6},{8,9},{9,8},{10,11... | collective-permute-start | bytes 2506760 | tf_op jit(solution)/shard_map/ppermute | solution.py:34
  44.1 39.0 %collective-permute-start.16 = (bf16[192,384]{1,0:T(8,128)(2,1)}, bf16[192,384]{1,0:T(8,128)(2,1)S(1)}, u32[]{:S(2)}, u32[]{:S(2)}) collective-permute-start(bf16[192,384]{1,0:T(8,128)(2,1)} %get-tuple-element.14), channel_id=1, source_target_pairs={{0,16},{8,24},{16,0},{24,8},{1,17},{9,25},{17,1},{25,9},{2,18},{10... | collective-permute-start | bytes 442376 | tf_op jit(solution)/shard_map/ppermute | solution.py:15
  56.4 44.2 %collective-permute-start.25 = (bf16[2,384,512]{2,1,0:T(8,128)(2,1)S(1)}, bf16[2,384,512]{2,1,0:T(8,128)(2,1)S(1)}, u32[]{:S(2)}, u32[]{:S(2)}) collective-permute-start(bf16[2,384,512]{2,1,0:T(8,128)(2,1)S(1)} %copy-done.34), channel_id=1, source_target_pairs={{0,8},{8,16},{16,24},{24,0},{1,9},{9,17},{17,25},{25,1},{2,10},{10... | collective-permute-start | bytes 2359304 | tf_op jit(solution)/shard_map/ppermute | solution.py:15
  63.0 78.5 %collective-permute-start.24 = (bf16[2,384,512]{2,1,0:T(8,128)(2,1)S(1)}, bf16[2,384,512]{2,1,0:T(8,128)(2,1)S(1)}, u32[]{:S(2)}, u32[]{:S(2)}) collective-permute-start(bf16[2,384,512]{2,1,0:T(8,128)(2,1)S(1)} %copy-done.34), channel_id=1, source_target_pairs={{0,16},{8,24},{16,0},{24,8},{1,17},{9,25},{17,1},{25,9},{2,18},{10... | collective-permute-start | bytes 2359304 | tf_op jit(solution)/shard_map/ppermute | solution.py:15
  83.1 32.0 %collective-permute-start.23 = (bf16[2,384,512]{2,1,0:T(8,128)(2,1)S(1)}, bf16[2,384,512]{2,1,0:T(8,128)(2,1)S(1)}, u32[]{:S(2)}, u32[]{:S(2)}) collective-permute-start(bf16[2,384,512]{2,1,0:T(8,128)(2,1)S(1)} %copy-done.34), channel_id=1, source_target_pairs={{0,24},{8,0},{16,8},{24,16},{1,25},{9,1},{17,9},{25,17},{2,26},{10... | collective-permute-start | bytes 2359304 | tf_op jit(solution)/shard_map/ppermute | solution.py:15
  89.7 52.7 %collective-permute-start.13 = (bf16[272,1536]{1,0:T(8,128)(2,1)}, bf16[272,1536]{1,0:T(8,128)(2,1)S(1)}, u32[]{:S(2)}, u32[]{:S(2)}) collective-permute-start(bf16[272,1536]{1,0:T(8,128)(2,1)} %collective-permute-done.12), channel_id=1, source_target_pairs={{0,1},{1,0},{2,3},{3,2},{4,5},{5,4},{6,7},{7,6},{8,9},{9,8},{10,11... | collective-permute-start | bytes 2506760 | tf_op jit(solution)/shard_map/ppermute | solution.py:34
  98.5 204.6 %collective-permute-start.36 = (bf16[272,1536]{1,0:T(8,128)(2,1)}, bf16[272,1536]{1,0:T(8,128)(2,1)}, u32[]{:S(2)}, u32[]{:S(2)}) collective-permute-start(bf16[272,1536]{1,0:T(8,128)(2,1)} %fusion.60), channel_id=1, source_target_pairs={{0,1},{1,0},{2,3},{3,2},{4,5},{5,4},{6,7},{7,6},{8,9},{9,8},{10,11... | collective-permute-start | bytes 2506760 | tf_op jit(solution)/shard_map/ppermute | solution.py:34
  100.6 64.8 %collective-permute-start.10 = (bf16[3,1152,192]{1,2,0:T(8,128)(2,1)S(1)}, bf16[3,1152,192]{1,2,0:T(8,128)(2,1)S(1)}, u32[]{:S(2)}, u32[]{:S(2)}) collective-permute-start(bf16[3,1152,192]{1,2,0:T(8,128)(2,1)S(1)} %pad_maximum_fusion.24), channel_id=1, source_target_pairs={{0,4},{2,6},{4,0},{6,2},{1,5},{3,7},{5,1},{7,3},{8,12},{10,14},{12... | collective-permute-start | bytes 3981320 | tf_op jit(solution)/shard_map/ppermute | solution.py:24
  115.1 32.0 %collective-permute-start.31 = (bf16[512,384]{1,0:T(8,128)(2,1)S(1)}, bf16[512,384]{1,0:T(8,128)(2,1)S(1)}, u32[]{:S(2)}, u32[]{:S(2)}) collective-permute-start(bf16[512,384]{1,0:T(8,128)(2,1)S(1)} %copy-done.46), channel_id=1, source_target_pairs={{0,8},{8,16},{16,24},{24,0},{1,9},{9,17},{17,25},{25,1},{2,10},{10... | collective-permute-start | bytes 1179656 | tf_op jit(solution)/shard_map/ppermute | solution.py:15
  147.1 46.3 %collective-permute-start.9 = (bf16[3,1536,192]{1,2,0:T(8,128)(2,1)S(1)}, bf16[3,1536,192]{1,2,0:T(8,128)(2,1)S(1)}, u32[]{:S(2)}, u32[]{:S(2)}) collective-permute-start(bf16[3,1536,192]{1,2,0:T(8,128)(2,1)S(1)} %pad_maximum_fusion.13), channel_id=1, source_target_pairs={{0,2},{2,0},{4,6},{6,4},{1,3},{3,1},{5,7},{7,5},{8,10},{10,8},{12,... | collective-permute-start | bytes 5308424 | tf_op jit(solution)/shard_map/ppermute | solution.py:28
  161.6 31.3 %collective-permute-start.14 = (bf16[544,1536]{1,0:T(8,128)(2,1)S(1)}, bf16[544,1536]{1,0:T(8,128)(2,1)S(1)}, u32[]{:S(2)}, u32[]{:S(2)}) collective-permute-start(bf16[544,1536]{1,0:T(8,128)(2,1)S(1)} %maximum_select_fusion), channel_id=1, source_target_pairs={{0,2},{2,0},{4,6},{6,4},{1,3},{3,1},{5,7},{7,5},{8,10},{10,8},{12,... | collective-permute-start | bytes 5013512 | tf_op jit(solution)/shard_map/ppermute | solution.py:28
  163.2 23.8 %collective-permute-start.33 = (bf16[512,1152]{1,0:T(8,128)(2,1)S(1)}, bf16[512,1152]{1,0:T(8,128)(2,1)S(1)}, u32[]{:S(2)}, u32[]{:S(2)}) collective-permute-start(bf16[512,1152]{1,0:T(8,128)(2,1)S(1)} %pad_maximum_fusion.25), channel_id=1, source_target_pairs={{0,4},{2,6},{4,0},{6,2},{1,5},{3,7},{5,1},{7,3},{8,12},{10,14},{12... | collective-permute-start | bytes 3538952 | tf_op jit(solution)/shard_map/ppermute | solution.py:24
  165.6 29.1 %collective-permute-start.11 = (bf16[3,1536,192]{1,2,0:T(8,128)(2,1)S(1)}, bf16[3,1536,192]{1,2,0:T(8,128)(2,1)S(1)}, u32[]{:S(2)}, u32[]{:S(2)}) collective-permute-start(bf16[3,1536,192]{1,2,0:T(8,128)(2,1)S(1)} %pad_maximum_fusion.14), channel_id=1, source_target_pairs={{0,2},{2,0},{4,6},{6,4},{1,3},{3,1},{5,7},{7,5},{8,10},{10,8},{12,... | collective-permute-start | bytes 5308424 | tf_op jit(solution)/shard_map/ppermute | solution.py:28
  187.0 110.4 %collective-permute-start.18 = (bf16[192,1536]{1,0:T(8,128)(2,1)}, bf16[192,1536]{1,0:T(8,128)(2,1)}, u32[]{:S(2)}, u32[]{:S(2)}) collective-permute-start(bf16[192,1536]{1,0:T(8,128)(2,1)} %constant_dynamic-update-slice_fusion.5), channel_id=1, source_target_pairs={{0,2},{2,0},{4,6},{6,4},{1,3},{3,1},{5,7},{7,5},{8,10},{10,8},{12,... | collective-permute-start | bytes 1769480 | tf_op jit(solution)/shard_map/ppermute | solution.py:28
  192.9 104.8 %collective-permute-start.20 = (bf16[192,1536]{1,0:T(8,128)(2,1)}, bf16[192,1536]{1,0:T(8,128)(2,1)}, u32[]{:S(2)}, u32[]{:S(2)}) collective-permute-start(bf16[192,1536]{1,0:T(8,128)(2,1)} %pad_maximum_fusion.34), channel_id=1, source_target_pairs={{0,2},{2,0},{4,6},{6,4},{1,3},{3,1},{5,7},{7,5},{8,10},{10,8},{12,... | collective-permute-start | bytes 1769480 | tf_op jit(solution)/shard_map/ppermute | solution.py:28
  193.4 108.3 %collective-permute-start.27 = (bf16[2,1152,512]{2,1,0:T(8,128)(2,1)}, bf16[2,1152,512]{2,1,0:T(8,128)(2,1)S(1)}, u32[]{:S(2)}, u32[]{:S(2)}) collective-permute-start(bf16[2,1152,512]{2,1,0:T(8,128)(2,1)} %pad_maximum_fusion.11), channel_id=1, source_target_pairs={{0,4},{2,6},{4,0},{6,2},{1,5},{3,7},{5,1},{7,3},{8,12},{10,14},{12... | collective-permute-start | bytes 7077896 | tf_op jit(solution)/shard_map/ppermute | solution.py:24
  194.6 147.2 %collective-permute-start.26 = (bf16[2,1536,512]{2,1,0:T(8,128)(2,1)}, bf16[2,1536,512]{2,1,0:T(8,128)(2,1)}, u32[]{:S(2)}, u32[]{:S(2)}) collective-permute-start(bf16[2,1536,512]{2,1,0:T(8,128)(2,1)} %constant_dynamic-update-slice_fusion.9), channel_id=1, source_target_pairs={{0,2},{2,0},{4,6},{6,4},{1,3},{3,1},{5,7},{7,5},{8,10},{10,8},{12,... | collective-permute-start | bytes 9437192 | tf_op jit(solution)/shard_map/ppermute | solution.py:28
  297.4 26.1 %collective-permute-start.32 = (bf16[512,1536]{1,0:T(8,128)(2,1)}, bf16[512,1536]{1,0:T(8,128)(2,1)}, u32[]{:S(2)}, u32[]{:S(2)}) collective-permute-start(bf16[512,1536]{1,0:T(8,128)(2,1)} %copy-done.75), channel_id=1, source_target_pairs={{0,2},{2,0},{4,6},{6,4},{1,3},{3,1},{5,7},{7,5},{8,10},{10,8},{12,... | collective-permute-start | bytes 4718600 | tf_op jit(solution)/shard_map/ppermute | solution.py:28
  297.7 25.7 %collective-permute-start.34 = (bf16[512,1536]{1,0:T(8,128)(2,1)}, bf16[512,1536]{1,0:T(8,128)(2,1)}, u32[]{:S(2)}, u32[]{:S(2)}) collective-permute-start(bf16[512,1536]{1,0:T(8,128)(2,1)} %pad_maximum_fusion.21), channel_id=1, source_target_pairs={{0,2},{2,0},{4,6},{6,4},{1,3},{3,1},{5,7},{7,5},{8,10},{10,8},{12,... | collective-permute-start | bytes 4718600 | tf_op jit(solution)/shard_map/ppermute | solution.py:28
  303.1 38.7 %collective-permute-start.28 = (bf16[2,1536,512]{2,1,0:T(8,128)(2,1)S(1)}, bf16[2,1536,512]{2,1,0:T(8,128)(2,1)S(1)}, u32[]{:S(2)}, u32[]{:S(2)}) collective-permute-start(bf16[2,1536,512]{2,1,0:T(8,128)(2,1)S(1)} %pad_maximum_fusion.7), channel_id=1, source_target_pairs={{0,2},{2,0},{4,6},{6,4},{1,3},{3,1},{5,7},{7,5},{8,10},{10,8},{12,... | collective-permute-start | bytes 9437192 | tf_op jit(solution)/shard_map/ppermute | solution.py:28
  409.8 39.1 %collective-permute-start.35 = (bf16[272,1536]{1,0:T(8,128)(2,1)S(1)}, bf16[272,1536]{1,0:T(8,128)(2,1)S(1)}, u32[]{:S(2)}, u32[]{:S(2)}) collective-permute-start(bf16[272,1536]{1,0:T(8,128)(2,1)S(1)} %dynamic-slice_convert_fusion.3), channel_id=1, source_target_pairs={{0,1},{1,0},{2,3},{3,2},{4,5},{5,4},{6,7},{7,6},{8,9},{9,8},{10,11... | collective-permute-start | bytes 2506760 | tf_op jit(solution)/shard_map/ppermute | solution.py:51
  435.1 155.3 %collective-permute-start.67 = (bf16[2,512,1536]{2,1,0:T(8,128)(2,1)}, bf16[2,512,1536]{2,1,0:T(8,128)(2,1)}, u32[]{:S(2)}, u32[]{:S(2)}) collective-permute-start(bf16[2,512,1536]{2,1,0:T(8,128)(2,1)} %pad_maximum_fusion.8), channel_id=1, source_target_pairs={{0,2},{2,0},{4,6},{6,4},{1,3},{3,1},{5,7},{7,5},{8,10},{10,8},{12,... | collective-permute-start | bytes 9437192 | tf_op jit(solution)/shard_map/ppermute | solution.py:28
  456.0 193.8 %collective-permute-start.59 = (bf16[2,2,1536,512]{3,2,1,0:T(8,128)(2,1)}, bf16[2,2,1536,512]{3,2,1,0:T(8,128)(2,1)}, u32[]{:S(2)}, u32[]{:S(2)}) collective-permute-start(bf16[2,2,1536,512]{3,2,1,0:T(8,128)(2,1)} %pad_maximum_fusion.4), channel_id=1, source_target_pairs={{0,2},{2,0},{4,6},{6,4},{1,3},{3,1},{5,7},{7,5},{8,10},{10,8},{12,... | collective-permute-start | bytes 18874376 | tf_op jit(solution)/shard_map/ppermute | solution.py:28
  548.2 39.6 %collective-permute-start.51 = (bf16[2,192,1536]{2,1,0:T(8,128)(2,1)}, bf16[2,192,1536]{2,1,0:T(8,128)(2,1)}, u32[]{:S(2)}, u32[]{:S(2)}) collective-permute-start(bf16[2,192,1536]{2,1,0:T(8,128)(2,1)} %pad_maximum_fusion.26), channel_id=1, source_target_pairs={{0,2},{2,0},{4,6},{6,4},{1,3},{3,1},{5,7},{7,5},{8,10},{10,8},{12,... | collective-permute-start | bytes 3538952 | tf_op jit(solution)/shard_map/ppermute | solution.py:28
  587.3 68.5 %collective-permute-start.43 = (bf16[2,3,1536,192]{2,3,1,0:T(8,128)(2,1)S(1)}, bf16[2,3,1536,192]{2,3,1,0:T(8,128)(2,1)S(1)}, u32[]{:S(2)}, u32[]{:S(2)}) collective-permute-start(bf16[2,3,1536,192]{2,3,1,0:T(8,128)(2,1)S(1)} %pad_maximum_fusion.5), channel_id=1, source_target_pairs={{0,2},{2,0},{4,6},{6,4},{1,3},{3,1},{5,7},{7,5},{8,10},{10,8},{12,... | collective-permute-start | bytes 10616840 | tf_op jit(solution)/shard_map/ppermute | solution.py:28
  624.2 24.0 %collective-permute-start.41 = (bf16[272,1536]{1,0:T(8,128)(2,1)}, bf16[272,1536]{1,0:T(8,128)(2,1)S(1)}, u32[]{:S(2)}, u32[]{:S(2)}) collective-permute-start(bf16[272,1536]{1,0:T(8,128)(2,1)} %dynamic-slice_convert_fusion), channel_id=1, source_target_pairs={{0,1},{1,0},{2,3},{3,2},{4,5},{5,4},{6,7},{7,6},{8,9},{9,8},{10,11... | collective-permute-start | bytes 2506760 | tf_op jit(solution)/shard_map/ppermute | solution.py:51
  644.4 35.6 %collective-permute-start.68 = (bf16[512,1536]{1,0:T(8,128)(2,1)S(1)}, bf16[512,1536]{1,0:T(8,128)(2,1)S(1)}, u32[]{:S(2)}, u32[]{:S(2)}) collective-permute-start(bf16[512,1536]{1,0:T(8,128)(2,1)S(1)} %copy-done.47), channel_id=1, source_target_pairs={{0,4},{2,6},{4,0},{6,2},{1,5},{3,7},{5,1},{7,3},{8,12},{10,14},{12... | collective-permute-start | bytes 4718600 | tf_op jit(solution)/shard_map/ppermute | solution.py:24
  645.0 38.6 %collective-permute-start.40 = (bf16[272,1536]{1,0:T(8,128)(2,1)S(1)}, bf16[272,1536]{1,0:T(8,128)(2,1)S(1)}, u32[]{:S(2)}, u32[]{:S(2)}) collective-permute-start(bf16[272,1536]{1,0:T(8,128)(2,1)S(1)} %dynamic-slice_convert_fusion.1), channel_id=1, source_target_pairs={{0,1},{1,0},{2,3},{3,2},{4,5},{5,4},{6,7},{7,6},{8,9},{9,8},{10,11... | collective-permute-start | bytes 2506760 | tf_op jit(solution)/shard_map/ppermute | solution.py:51
  648.5 49.6 %collective-permute-start.42 = (bf16[272,1536]{1,0:T(8,128)(2,1)S(1)}, bf16[272,1536]{1,0:T(8,128)(2,1)S(1)}, u32[]{:S(2)}, u32[]{:S(2)}) collective-permute-start(bf16[272,1536]{1,0:T(8,128)(2,1)S(1)} %add_convert_fusion.4), channel_id=1, source_target_pairs={{4,0},{6,2},{5,1},{7,3},{12,8},{14,10},{13,9},{15,11},{20,16},{22,... | collective-permute-start | bytes 2506760 | tf_op jit(solution)/shard_map/ppermute | solution.py:154
  653.6 192.2 %collective-permute-start.60 = (bf16[2,1536,512]{2,1,0:T(8,128)(2,1)}, bf16[2,1536,512]{2,1,0:T(8,128)(2,1)}, u32[]{:S(2)}, u32[]{:S(2)}) collective-permute-start(bf16[2,1536,512]{2,1,0:T(8,128)(2,1)} %fusion.12), channel_id=1, source_target_pairs={{0,4},{2,6},{4,0},{6,2},{1,5},{3,7},{5,1},{7,3},{8,12},{10,14},{12... | collective-permute-start | bytes 9437192 | tf_op jit(solution)/shard_map/ppermute | solution.py:24
  657.8 181.4 %collective-permute-start.44 = (bf16[3,1536,192]{1,2,0:T(8,128)(2,1)}, bf16[3,1536,192]{1,2,0:T(8,128)(2,1)}, u32[]{:S(2)}, u32[]{:S(2)}) collective-permute-start(bf16[3,1536,192]{1,2,0:T(8,128)(2,1)} %fusion.21), channel_id=1, source_target_pairs={{0,4},{2,6},{4,0},{6,2},{1,5},{3,7},{5,1},{7,3},{8,12},{10,14},{12... | collective-permute-start | bytes 5308424 | tf_op jit(solution)/shard_map/ppermute | solution.py:24
  683.5 152.0 %collective-permute-start.69 = (bf16[512,384]{1,0:T(8,128)(2,1)}, bf16[512,384]{1,0:T(8,128)(2,1)}, u32[]{:S(2)}, u32[]{:S(2)}) collective-permute-start(bf16[512,384]{1,0:T(8,128)(2,1)} %get-tuple-element.126), channel_id=1, source_target_pairs={{0,8},{8,16},{16,24},{24,0},{1,9},{9,17},{17,25},{25,1},{2,10},{10... | collective-permute-start | bytes 1179656 | tf_op jit(solution)/shard_map/ppermute | solution.py:20
  683.5 152.0 %collective-permute-start.71 = (bf16[512,384]{1,0:T(8,128)(2,1)S(1)}, bf16[512,384]{1,0:T(8,128)(2,1)}, u32[]{:S(2)}, u32[]{:S(2)}) collective-permute-start(bf16[512,384]{1,0:T(8,128)(2,1)S(1)} %get-tuple-element.127), channel_id=1, source_target_pairs={{0,24},{8,0},{16,8},{24,16},{1,25},{9,1},{17,9},{25,17},{2,26},{10... | collective-permute-start | bytes 1179656 | tf_op jit(solution)/shard_map/ppermute | solution.py:20
  698.0 137.5 %collective-permute-start.70 = (bf16[512,384]{1,0:T(8,128)(2,1)S(1)}, bf16[512,384]{1,0:T(8,128)(2,1)}, u32[]{:S(2)}, u32[]{:S(2)}) collective-permute-start(bf16[512,384]{1,0:T(8,128)(2,1)S(1)} %get-tuple-element.128), channel_id=1, source_target_pairs={{0,16},{8,24},{16,0},{24,8},{1,17},{9,25},{17,1},{25,9},{2,18},{10... | collective-permute-start | bytes 1179656 | tf_op jit(solution)/shard_map/ppermute | solution.py:20
  845.9 53.9 %collective-permute-start.46 = (bf16[3,384,192]{1,2,0:T(8,128)(2,1)S(1)}, bf16[3,384,192]{1,2,0:T(8,128)(2,1)S(1)}, u32[]{:S(2)}, u32[]{:S(2)}) collective-permute-start(bf16[3,384,192]{1,2,0:T(8,128)(2,1)S(1)} %get-tuple-element.110), channel_id=1, source_target_pairs={{0,16},{8,24},{16,0},{24,8},{1,17},{9,25},{17,1},{25,9},{2,18},{10... | collective-permute-start | bytes 1327112 | tf_op jit(solution)/shard_map/ppermute | solution.py:20
  850.3 52.4 %collective-permute-start.61 = (bf16[2,384,512]{2,1,0:T(8,128)(2,1)S(1)}, bf16[2,384,512]{2,1,0:T(8,128)(2,1)S(1)}, u32[]{:S(2)}, u32[]{:S(2)}) collective-permute-start(bf16[2,384,512]{2,1,0:T(8,128)(2,1)S(1)} %get-tuple-element.93), channel_id=1, source_target_pairs={{0,8},{8,16},{16,24},{24,0},{1,9},{9,17},{17,25},{25,1},{2,10},{10... | collective-permute-start | bytes 2359304 | tf_op jit(solution)/shard_map/ppermute | solution.py:20
  850.8 54.7 %collective-permute-start.63 = (bf16[2,384,512]{2,1,0:T(8,128)(2,1)S(1)}, bf16[2,384,512]{2,1,0:T(8,128)(2,1)S(1)}, u32[]{:S(2)}, u32[]{:S(2)}) collective-permute-start(bf16[2,384,512]{2,1,0:T(8,128)(2,1)S(1)} %get-tuple-element.94), channel_id=1, source_target_pairs={{0,24},{8,0},{16,8},{24,16},{1,25},{9,1},{17,9},{25,17},{2,26},{10... | collective-permute-start | bytes 2359304 | tf_op jit(solution)/shard_map/ppermute | solution.py:20
  854.2 96.1 %collective-permute-start.62 = (bf16[2,384,512]{2,1,0:T(8,128)(2,1)S(1)}, bf16[2,384,512]{2,1,0:T(8,128)(2,1)S(1)}, u32[]{:S(2)}, u32[]{:S(2)}) collective-permute-start(bf16[2,384,512]{2,1,0:T(8,128)(2,1)S(1)} %get-tuple-element.95), channel_id=1, source_target_pairs={{0,16},{8,24},{16,0},{24,8},{1,17},{9,25},{17,1},{25,9},{2,18},{10... | collective-permute-start | bytes 2359304 | tf_op jit(solution)/shard_map/ppermute | solution.py:20
  862.4 92.7 %collective-permute-start.74 = (bf16[512,384]{1,0:T(8,128)(2,1)S(1)}, bf16[512,384]{1,0:T(8,128)(2,1)S(1)}, u32[]{:S(2)}, u32[]{:S(2)}) collective-permute-start(bf16[512,384]{1,0:T(8,128)(2,1)S(1)} %add_convert_fusion.10), channel_id=1, source_target_pairs={{0,2},{2,0},{4,6},{6,4},{1,3},{3,1},{5,7},{7,5},{8,10},{10,8},{12,... | collective-permute-start | bytes 1179656 | tf_op jit(solution)/shard_map/ppermute | solution.py:28
  899.8 55.4 %collective-permute-start.73 = (bf16[512,384]{1,0:T(8,128)(2,1)S(1)}, bf16[512,384]{1,0:T(8,128)(2,1)S(1)}, u32[]{:S(2)}, u32[]{:S(2)}) collective-permute-start(bf16[512,384]{1,0:T(8,128)(2,1)S(1)} %collective-permute-done.72), channel_id=1, source_target_pairs={{0,2},{2,0},{4,6},{6,4},{1,3},{3,1},{5,7},{7,5},{8,10},{10,8},{12,... | collective-permute-start | bytes 1179656 | tf_op jit(solution)/shard_map/ppermute | solution.py:28
  902.7 52.4 %collective-permute-start.48 = (bf16[3,384,192]{1,2,0:T(8,128)(2,1)S(1)}, bf16[3,384,192]{1,2,0:T(8,128)(2,1)S(1)}, u32[]{:S(2)}, u32[]{:S(2)}) collective-permute-start(bf16[3,384,192]{1,2,0:T(8,128)(2,1)S(1)} %add_convert_fusion.9), channel_id=1, source_target_pairs={{0,4},{2,6},{4,0},{6,2},{1,5},{3,7},{5,1},{7,3},{8,12},{10,14},{12... | collective-permute-start | bytes 1327112 | tf_op jit(solution)/shard_map/ppermute | solution.py:24
  (123 other events, 2939.7 us)
where the time goes:
time: 990 us; the launch traced here: 983 us
  matrix products  238 us (24%)
  waiting for transfers between devices  233 us (24%)
  starting transfers between devices  184 us (19%)
  other arithmetic  144 us (15%)
  blocking collectives  136 us (14%)
  local copies, waits for them, and re-layouts  46.6 us (5%)
    psum x1, blocking collectives, shards(): lax.psum(to_natural(jnp.stack([gain_one_grad, gain_two_grad])), ('fsdp',...  136 us
    ppermute x12, waiting for transfers between devices, push_fsdp(): lax.ppermute(values, 'fsdp', [(i, (i + step) % count) for i in range(coun...  89.4 us
    ppermute x15, starting transfers between devices, pull_fsdp(): lax.ppermute(values, 'fsdp', [(i, (i - step) % count) for i in range(coun...  72.6 us
    ppermute x12, waiting for transfers between devices, swap_chip(): lax.ppermute(values, 'ctx', [(i, i ^ 2) for i in range(lax.axis_size('ctx...  63.1 us
    ppermute x23, starting transfers between devices, swap_core(): lax.ppermute(values, 'ctx', [(i, i ^ 1) for i in range(lax.axis_size('ctx...  54.2 us
    dot_general x7, matrix products, dot_nt(): lax.dot_general(left, right, (((1,), (1,)), ((), ())), preferred_element_...  51.7 us
    dot_general x7, matrix products, dot(): return jnp.dot(left, right, preferred_element_type=F32)  41.6 us
    dot_general x7, matrix products, dot_tn(): lax.dot_general(left, right, (((0,), (0,)), ((), ())), preferred_element_...  34.6 us
  transfers between devices with their start and end apart: 75, of which 22 were waited for; matrix products, arithmetic and copies ran while one was open for 36% of the time, Pallas kernels for 0%

commit v1 on v0

--- a/solution.py
+++ b/solution.py
@@ -314,8 +314,11 @@
     normed_grad = return_window(far, near, own + dot_nt(query_low, qkv_whole[0]))
     gain_one_grad = jnp.sum(normed_grad * inputs * inv_one, axis=0)
     grad_input = resid_grad + normalize_back(inputs, inv_one, gain_one, normed_grad)
-    gain_grads = lax.psum(
-        to_natural(jnp.stack([gain_one_grad, gain_two_grad])), ("fsdp", "ctx", "tp")
+    gain_grads = jnp.sum(
+        lax.all_gather(
+            to_natural(jnp.stack([gain_one_grad, gain_two_grad])), ("fsdp", "ctx", "tp")
+        ),
+        axis=0,
     )
     gain_rows = gain_attn.shape[0]
     gain_own = lax.dynamic_slice_in_dim(

time: 990 us -> 1010 us (1.020)
  blocking collectives: 136 us -> 158 us
    all_gather x0 -> x1, blocking collectives: none -> 158 us  [shards(): lax.all_gather(to_natural(jnp.stack([gain_one_grad, gain_two_grad])), ('f...]
    psum x1 -> x0, blocking collectives: 136 us -> none  [shards(): lax.psum(to_natural(jnp.stack([gain_one_grad, gain_two_grad])), ('fsdp',...]
    ppermute x23, starting transfers between devices: 54.2 us -> 34.7 us  [swap_core(): lax.ppermute(values, 'ctx', [(i, i ^ 1) for i in range(lax.axis_size('ctx...]
    ppermute x12, starting transfers between devices: 25.1 us -> 39.7 us  [push_fsdp(): lax.ppermute(values, 'fsdp', [(i, (i + step) % count) for i in range(coun...]
  transfers between devices with their start and end apart: 75 -> 75, of which waited for: 22 -> 20; matrix products, arithmetic and copies ran while one was open for 36% -> 35% of each run, Pallas kernels for 0% -> 0%
where the time goes in v1:
time: 1010 us; the launch traced here: 1000 us
  matrix products  238 us (24%)
  waiting for transfers between devices  235 us (23%)
  starting transfers between devices  177 us (18%)
  blocking collectives  158 us (16%)
  other arithmetic  144 us (14%)
  local copies, waits for them, and re-layouts  46.8 us (5%)
    all_gather x1, blocking collectives, shards(): lax.all_gather(to_natural(jnp.stack([gain_one_grad, gain_two_grad])), ('f...  158 us
    ppermute x12, waiting for transfers between devices, push_fsdp(): lax.ppermute(values, 'fsdp', [(i, (i + step) % count) for i in range(coun...  88 us
    ppermute x15, starting transfers between devices, pull_fsdp(): lax.ppermute(values, 'fsdp', [(i, (i - step) % count) for i in range(coun...  72.6 us
    ppermute x12, waiting for transfers between devices, swap_chip(): lax.ppermute(values, 'ctx', [(i, i ^ 2) for i in range(lax.axis_size('ctx...  67.1 us
    dot_general x7, matrix products, dot_nt(): lax.dot_general(left, right, (((1,), (1,)), ((), ())), preferred_element_...  51.7 us
    dot_general x7, matrix products, dot(): return jnp.dot(left, right, preferred_element_type=F32)  41.6 us
    ppermute x12, starting transfers between devices, push_fsdp(): lax.ppermute(values, 'fsdp', [(i, (i + step) % count) for i in range(coun...  39.7 us
    ppermute x23, starting transfers between devices, swap_core(): lax.ppermute(values, 'ctx', [(i, i ^ 1) for i in range(lax.axis_size('ctx...  34.7 us
  transfers between devices with their start and end apart: 75, of which 20 were waited for; matrix products, arithmetic and copies ran while one was open for 35% of the time, Pallas kernels for 0%

profile of v1, /device:TPU:1, one launch (start us, length us, event | category | flops | bytes accessed | tf_op | source)
XLA Modules:
  0.0 1001.1 jit_solution(7110836993346961025)
XLA Ops:
  45.6 9.8 collective-permute-start.15
  58.1 4.9 collective-permute-done.15
  63.0 19.4 %collective-permute-start.24 = (bf16[2,384,512]{2,1,0:T(8,128)(2,1)S(1)}, bf16[2,384,512]{2,1,0:T(8,128)(2,1)S(1)}, u32[]{:S(2)}, u32[]{:S(2)}) collective-permute-start(bf16[2,384,512]{2,1,0:T(8,128)(2,1)S(1)} %copy-done.34), channel_id=1, source_target_pairs={{0,16},{8,24},{16,0},{24,8},{1,17},{9,25},{17,1},{25,9},{2,18},{10... | collective-permute-start | bytes 2359304 | tf_op jit(solution)/shard_map/ppermute | solution.py:15
  92.5 6.0 collective-permute-done.19
  101.8 13.3 %collective-permute-done.23 = bf16[2,384,512]{2,1,0:T(8,128)(2,1)S(1)} collective-permute-done((bf16[2,384,512]{2,1,0:T(8,128)(2,1)S(1)}, bf16[2,384,512]{2,1,0:T(8,128)(2,1)S(1)}, u32[]{:S(2)}, u32[]{:S(2)}) %collective-permute-start.23) | collective-permute-done | bytes 786464 | tf_op jit(solution)/shard_map/ppermute | solution.py:15
  115.1 25.5 %collective-permute-start.31 = (bf16[512,384]{1,0:T(8,128)(2,1)S(1)}, bf16[512,384]{1,0:T(8,128)(2,1)S(1)}, u32[]{:S(2)}, u32[]{:S(2)}) collective-permute-start(bf16[512,384]{1,0:T(8,128)(2,1)S(1)} %copy-done.46), channel_id=1, source_target_pairs={{0,8},{8,16},{16,24},{24,0},{1,9},{9,17},{17,25},{25,1},{2,10},{10... | collective-permute-start | bytes 1179656 | tf_op jit(solution)/shard_map/ppermute | solution.py:15
  147.1 6.1 collective-permute-start.9
  153.2 8.4 collective-permute-done.30
  171.5 15.6 %collective-permute-done.33 = bf16[512,1152]{1,0:T(8,128)(2,1)S(1)} collective-permute-done((bf16[512,1152]{1,0:T(8,128)(2,1)S(1)}, bf16[512,1152]{1,0:T(8,128)(2,1)S(1)}, u32[]{:S(2)}, u32[]{:S(2)}) %collective-permute-start.33) | collective-permute-done | bytes 1179680 | tf_op jit(solution)/shard_map/ppermute | solution.py:24
  195.5 11.4 %pad_maximum_fusion.1 = bf16[3,1536,768]{1,2,0:T(8,128)(2,1)S(1)} fusion(bf16[3,1536,192]{1,2,0:T(8,128)(2,1)S(1)} %collective-permute-done.11, bf16[3,1152,192]{1,2,0:T(8,128)(2,1)S(1)} %collective-permute-done.10, bf16[3,384,192]{1,2,0:T(8,128)(2,1)S(1)} %copy-done.22, bf16[3,1536,192]{1,2,0:T(8,128)(2,1)S(1)} %collective-permute-done.9, ...), kind=kLoop, calls=%fused_computation.23 | loop fusion | flops 56623104 | bytes 14155776 | tf_op jit(solution)/shard_map/concatenate | solution.py:219
  212.2 5.3 convolution_convert_fusion.7
  221.9 7.7 fusion.18
  233.0 20.2 %fusion.3 = (f32[12,544]{1,0:T(8,128)S(1)}, f32[12,544,1632]{2,1,0:T(8,128)}) fusion(pred[544,1632]{1,0:T(8,128)(4,1)} %and_and_fusion, bf16[1632,12,32]{0,2,1:T(8,128)(2,1)} %get-tuple-element.85, bf16[1632,12,32]{0,2,1:T(8,128)(2,1)} %get-tuple-element.84, bf16[544,12,32]{0,2,1:T(8,128)(2,1)} %get-tuple-element.103, ...), kind=kOutput, calls=%fused_computation.7 | convolution fusion | flops 1402312320 | bytes 46871040 | tf_op jit(solution)/shard_map/qhd,khd->hqk/dot_general | solution.py:254
  253.2 23.3 %fusion = f32[12,544]{1,0:T(8,128)S(1)} fusion(f32[12,544,1632]{2,1,0:T(8,128)} %get-tuple-element.150, f32[12,544]{1,0:T(8,128)S(1)} %get-tuple-element.149, pred[544,1632]{1,0:T(8,128)(4,1)} %and_and_fusion), kind=kLoop, calls=%fused_computation.4 | loop fusion | flops 53261952 | bytes 43554816 | tf_op jit(solution)/shard_map/reduce_sum | solution.py:258
  276.5 20.9 %fusion.66 = (bf16[544,12,64]{0,2,1:T(8,128)(2,1)}, f32[12,544,64]{1,2,0:T(8,128)}) fusion(f32[544,12]{0,1:T(8,128)S(1)} %bitcast.198, bf16[1632,12,64]{0,2,1:T(8,128)(2,1)} %bitcast.184, f32[12,544,1632]{2,1,0:T(8,128)} %get-tuple-element.150, f32[12,544]{1,0:T(8,128)S(1)} %get-tuple-element.149, pred[544,1632]{1,0:T(8,128)(4,1)} %and_and_fusion), kind=kOutput, calls=%fused_computation.216 | convolution fusion | flops 1417777152 | bytes 48568320 | tf_op jit(solution)/shard_map/hqk,khd->hqd/dot_general | solution.py:259
  305.8 15.9 %collective-permute-done.21 = bf16[272,1536]{1,0:T(8,128)(2,1)S(1)} collective-permute-done((bf16[272,1536]{1,0:T(8,128)(2,1)S(1)}, bf16[272,1536]{1,0:T(8,128)(2,1)S(1)}, u32[]{:S(2)}, u32[]{:S(2)}) %collective-permute-start.21) | collective-permute-done | bytes 835616 | tf_op jit(solution)/shard_map/ppermute | solution.py:51
  323.5 11.3 %fusion.59 = f32[544,2048]{1,0:T(8,128)} fusion(bf16[272,1536]{1,0:T(8,128)(2,1)S(1)} %get-tuple-element.117, bf16[272,1536]{1,0:T(8,128)(2,1)S(1)} %get-tuple-element.116, bf16[512,1536]{1,0:T(8,128)(2,1)} %collective-permute-done.34, bf16[512,1152]{1,0:T(8,128)(2,1)S(1)} %copy-done.51, bf16[512,384]{1,0:T(8,128)(2,1)S(1)} %copy-done.45, ...), kind=kOutput, calls=%fused_computation.184 | convolution fusion | flops 3457351680 | bytes 12419072 | tf_op jit(solution)/shard_map/dot_general | solution.py:198
  334.8 6.6 collective-permute-done.22
  341.9 28.1 %pad_maximum_fusion = bf16[2,1536,2048]{2,1,0:T(8,128)(2,1)S(1)} fusion(bf16[2,1536,512]{2,1,0:T(8,128)(2,1)S(1)} %collective-permute-done.28, bf16[2,1152,512]{2,1,0:T(8,128)(2,1)S(1)} %copy-done.7, bf16[2,384,512]{2,1,0:T(8,128)(2,1)S(1)} %copy-done.15, bf16[2,1536,512]{2,1,0:T(8,128)(2,1)} %collective-permute-done.26, ...), kind=kLoop, calls=%fused_computation.18 | loop fusion | flops 62914560 | bytes 25165824 | tf_op jit(solution)/shard_map/concatenate | solution.py:226
  370.0 5.8 fusion.17
  375.8 9.4 multiply_convert_fusion.2
  385.2 5.4 fusion.16
  390.7 5.4 fusion.11
  396.1 7.1 convolution_convert_fusion
  403.2 6.4 fusion.94
  411.4 7.2 fusion.10
  418.6 9.8 fusion.28
  437.5 10.7 %collective-permute-done.37 = bf16[272,1536]{1,0:T(8,128)(2,1)S(1)} collective-permute-done((bf16[272,1536]{1,0:T(8,128)(2,1)S(1)}, bf16[272,1536]{1,0:T(8,128)(2,1)S(1)}, u32[]{:S(2)}, u32[]{:S(2)}) %collective-permute-start.37) | collective-permute-done | bytes 835616 | tf_op jit(solution)/shard_map/ppermute | solution.py:51
  461.1 7.5 collective-permute-done.38
  478.1 19.7 %fusion.23 = bf16[12,64,1632]{2,1,0:T(8,128)(2,1)} fusion(bf16[544,12,64]{0,2,1:T(8,128)(2,1)S(1)} %bitcast.182, f32[12,544,1632]{2,1,0:T(8,128)} %get-tuple-element.150, f32[12,544]{1,0:T(8,128)S(1)} %log_add_fusion, pred[544,1632]{1,0:T(8,128)(4,1)S(1)} %copy-done.32), kind=kOutput, calls=%fused_computation.70 | convolution fusion | flops 1418194944 | bytes 46871040 | tf_op jit(solution)/shard_map/hqk,qhd->khd/dot_general | solution.py:293
  497.9 27.7 %multiply_convert_fusion = bf16[12,544,1632]{2,1,0:T(8,128)(2,1)} fusion(f32[12,544,1632]{2,1,0:T(8,128)} %get-tuple-element.150, bf16[544,12,64]{0,2,1:T(8,128)(2,1)} %bitcast.183, bf16[1632,12,64]{0,2,1:T(8,128)(2,1)} %bitcast.185, f32[12,544]{1,0:T(8,128)S(1)} %bitcast.202, f32[12,544]{1,0:T(8,128)S(1)} %log_add_fusion, pred[544,1632]{1,0:T(8,128)(4,1)} %and_and_fusion), kind=kOutput, calls=%fused_computation | convolution fusion | flops 1438248960 | bytes 68204544 | tf_op jit(solution)/shard_map/qhd,khd->hqk/dot_general | solution.py:289
  525.6 10.9 %multiply_bitcast_fusion.1 = f32[544,12,64]{0,2,1:T(8,128)S(1)} fusion(bf16[12,544,1632]{2,1,0:T(8,128)(2,1)} %multiply_convert_fusion, bf16[1632,12,32]{0,2,1:T(8,128)(2,1)S(1)} %copy-done.20, bf16[1632,12,32]{0,2,1:T(8,128)(2,1)S(1)} %copy-done.19), kind=kOutput, calls=%fused_computation.115 | convolution fusion | flops 1369104384 | bytes 25485312 | tf_op jit(solution)/shard_map/hqk,khd->qhd/dot_general | solution.py:291
  536.5 10.4 %multiply_bitcast_fusion = f32[1632,12,64]{0,2,1:T(8,128)S(1)} fusion(bf16[12,544,1632]{2,1,0:T(8,128)(2,1)} %multiply_convert_fusion, bf16[544,12,32]{0,2,1:T(8,128)(2,1)} %get-tuple-element.103, bf16[544,12,32]{0,2,1:T(8,128)(2,1)} %get-tuple-element.102), kind=kOutput, calls=%fused_computation.41 | convolution fusion | flops 1366597632 | bytes 27156480 | tf_op jit(solution)/shard_map/hqk,qhd->khd/dot_general | solution.py:292
  559.2 6.8 fusion.41
  565.9 9.2 convolution_add_fusion
  580.9 4.8 fusion.37
  596.9 7.6 collective-permute-done.52
  605.9 12.1 %collective-permute-start.53 = (bf16[192,384]{1,0:T(8,128)(2,1)S(1)}, bf16[192,384]{1,0:T(8,128)(2,1)S(1)}, u32[]{:S(2)}, u32[]{:S(2)}) collective-permute-start(bf16[192,384]{1,0:T(8,128)(2,1)S(1)} %get-tuple-element.135), channel_id=1, source_target_pairs={{0,8},{8,16},{16,24},{24,0},{1,9},{9,17},{17,25},{25,1},{2,10},{10... | collective-permute-start | bytes 442376 | tf_op jit(solution)/shard_map/ppermute | solution.py:20
  625.2 9.4 collective-permute-done.54
  635.6 6.3 fusion.26
  657.9 22.2 %collective-permute-done.68 = bf16[512,1536]{1,0:T(8,128)(2,1)S(1)} collective-permute-done((bf16[512,1536]{1,0:T(8,128)(2,1)S(1)}, bf16[512,1536]{1,0:T(8,128)(2,1)S(1)}, u32[]{:S(2)}, u32[]{:S(2)}) %collective-permute-start.68) | collective-permute-done | bytes 1572896 | tf_op jit(solution)/shard_map/ppermute | solution.py:24
  686.9 11.1 %collective-permute-done.42 = bf16[272,1536]{1,0:T(8,128)(2,1)S(1)} collective-permute-done((bf16[272,1536]{1,0:T(8,128)(2,1)S(1)}, bf16[272,1536]{1,0:T(8,128)(2,1)S(1)}, u32[]{:S(2)}, u32[]{:S(2)}) %collective-permute-start.42) | collective-permute-done | bytes 835616 | tf_op jit(solution)/shard_map/ppermute | solution.py:154
  699.1 157.7 %all-gather.1 = f32[32,2,1536]{2,1,0:T(2,128)S(1)} all-gather(f32[1,2,1536]{2,1,0:T(2,128)S(1)} %fusion.70), channel_id=2, replica_groups=mesh['fsdp'=4,'ctx'=4,'tp'=2] {'fsdp','ctx','tp'}, dimensions={0}, use_global_device_ids=true | all-gather | bytes 405504 | tf_op jit(solution)/shard_map/all_gather | solution.py:318
  874.3 14.4 %collective-permute-start.62 = (bf16[2,384,512]{2,1,0:T(8,128)(2,1)S(1)}, bf16[2,384,512]{2,1,0:T(8,128)(2,1)S(1)}, u32[]{:S(2)}, u32[]{:S(2)}) collective-permute-start(bf16[2,384,512]{2,1,0:T(8,128)(2,1)S(1)} %get-tuple-element.95), channel_id=1, source_target_pairs={{0,16},{8,24},{16,0},{24,8},{1,17},{9,25},{17,1},{25,9},{2,18},{10... | collective-permute-start | bytes 2359304 | tf_op jit(solution)/shard_map/ppermute | solution.py:20
  891.5 27.5 %collective-permute-done.46 = bf16[3,384,192]{1,2,0:T(8,128)(2,1)S(1)} collective-permute-done((bf16[3,384,192]{1,2,0:T(8,128)(2,1)S(1)}, bf16[3,384,192]{1,2,0:T(8,128)(2,1)S(1)}, u32[]{:S(2)}, u32[]{:S(2)}) %collective-permute-start.46) | collective-permute-done | bytes 442400 | tf_op jit(solution)/shard_map/ppermute | solution.py:20
  919.5 7.0 collective-permute-done.63
  926.4 41.9 %collective-permute-done.62 = bf16[2,384,512]{2,1,0:T(8,128)(2,1)S(1)} collective-permute-done((bf16[2,384,512]{2,1,0:T(8,128)(2,1)S(1)}, bf16[2,384,512]{2,1,0:T(8,128)(2,1)S(1)}, u32[]{:S(2)}, u32[]{:S(2)}) %collective-permute-start.62) | collective-permute-done | bytes 786464 | tf_op jit(solution)/shard_map/ppermute | solution.py:20
  973.8 15.7 %collective-permute-done.64 = bf16[2,384,512]{2,1,0:T(8,128)(2,1)} collective-permute-done((bf16[2,384,512]{2,1,0:T(8,128)(2,1)}, bf16[2,384,512]{2,1,0:T(8,128)(2,1)}, u32[]{:S(2)}, u32[]{:S(2)}) %collective-permute-start.64) | collective-permute-done | bytes 786464 | tf_op jit(solution)/shard_map/ppermute | solution.py:24
  (463 shorter events, 241.9 us)
Async XLA Ops:
  2.0 22.9 %collective-permute-start.4 = (bf16[2,384]{1,0:T(2,128)(2,1)S(1)}, bf16[2,384]{1,0:T(2,128)(2,1)S(1)}, u32[]{:S(2)}, u32[]{:S(2)}) collective-permute-start(bf16[2,384]{1,0:T(2,128)(2,1)S(1)} %pad_maximum_fusion.39), channel_id=1, source_target_pairs={{0,8},{8,16},{16,24},{24,0},{1,9},{9,17},{17,25},{25,1},{2,10},{10... | collective-permute-start | bytes 4616 | tf_op jit(solution)/shard_map/ppermute | solution.py:15
  4.2 23.7 %collective-permute-start.3 = (bf16[2,384]{1,0:T(2,128)(2,1)S(1)}, bf16[2,384]{1,0:T(2,128)(2,1)S(1)}, u32[]{:S(2)}, u32[]{:S(2)}) collective-permute-start(bf16[2,384]{1,0:T(2,128)(2,1)S(1)} %pad_maximum_fusion.39), channel_id=1, source_target_pairs={{0,16},{8,24},{16,0},{24,8},{1,17},{9,25},{17,1},{25,9},{2,18},{10... | collective-permute-start | bytes 4616 | tf_op jit(solution)/shard_map/ppermute | solution.py:15
  6.5 24.5 %collective-permute-start.2 = (bf16[2,384]{1,0:T(2,128)(2,1)S(1)}, bf16[2,384]{1,0:T(2,128)(2,1)S(1)}, u32[]{:S(2)}, u32[]{:S(2)}) collective-permute-start(bf16[2,384]{1,0:T(2,128)(2,1)S(1)} %pad_maximum_fusion.39), channel_id=1, source_target_pairs={{0,24},{8,0},{16,8},{24,16},{1,25},{9,1},{17,9},{25,17},{2,26},{10... | collective-permute-start | bytes 4616 | tf_op jit(solution)/shard_map/ppermute | solution.py:15
  12.1 31.7 %collective-permute-start.8 = (bf16[3,384,192]{1,2,0:T(8,128)(2,1)S(1)}, bf16[3,384,192]{1,2,0:T(8,128)(2,1)S(1)}, u32[]{:S(2)}, u32[]{:S(2)}) collective-permute-start(bf16[3,384,192]{1,2,0:T(8,128)(2,1)S(1)} %get-tuple-element.112), channel_id=1, source_target_pairs={{0,8},{8,16},{16,24},{24,0},{1,9},{9,17},{17,25},{25,1},{2,10},{10... | collective-permute-start | bytes 1327112 | tf_op jit(solution)/shard_map/ppermute | solution.py:15
  12.5 31.5 %collective-permute-start.7 = (bf16[3,384,192]{1,2,0:T(8,128)(2,1)S(1)}, bf16[3,384,192]{1,2,0:T(8,128)(2,1)S(1)}, u32[]{:S(2)}, u32[]{:S(2)}) collective-permute-start(bf16[3,384,192]{1,2,0:T(8,128)(2,1)S(1)} %get-tuple-element.112), channel_id=1, source_target_pairs={{0,16},{8,24},{16,0},{24,8},{1,17},{9,25},{17,1},{25,9},{2,18},{10... | collective-permute-start | bytes 1327112 | tf_op jit(solution)/shard_map/ppermute | solution.py:15
  35.8 52.6 %collective-permute-start.12 = (bf16[272,1536]{1,0:T(8,128)(2,1)}, bf16[272,1536]{1,0:T(8,128)(2,1)}, u32[]{:S(2)}, u32[]{:S(2)}) collective-permute-start(bf16[272,1536]{1,0:T(8,128)(2,1)} %fusion.46), channel_id=1, source_target_pairs={{0,4},{2,6},{1,5},{3,7},{8,12},{10,14},{9,13},{11,15},{16,20},{18,... | collective-permute-start | bytes 2506760 | tf_op jit(solution)/shard_map/ppermute | solution.py:143
  40.6 49.1 %collective-permute-start.5 = (bf16[272,1536]{1,0:T(8,128)(2,1)}, bf16[272,1536]{1,0:T(8,128)(2,1)}, u32[]{:S(2)}, u32[]{:S(2)}) collective-permute-start(bf16[272,1536]{1,0:T(8,128)(2,1)} %fusion.46), channel_id=1, source_target_pairs={{0,1},{1,0},{2,3},{3,2},{4,5},{5,4},{6,7},{7,6},{8,9},{9,8},{10,11... | collective-permute-start | bytes 2506760 | tf_op jit(solution)/shard_map/ppermute | solution.py:34
  44.1 39.0 %collective-permute-start.16 = (bf16[192,384]{1,0:T(8,128)(2,1)}, bf16[192,384]{1,0:T(8,128)(2,1)S(1)}, u32[]{:S(2)}, u32[]{:S(2)}) collective-permute-start(bf16[192,384]{1,0:T(8,128)(2,1)} %get-tuple-element.14), channel_id=1, source_target_pairs={{0,16},{8,24},{16,0},{24,8},{1,17},{9,25},{17,1},{25,9},{2,18},{10... | collective-permute-start | bytes 442376 | tf_op jit(solution)/shard_map/ppermute | solution.py:15
  56.4 44.2 %collective-permute-start.25 = (bf16[2,384,512]{2,1,0:T(8,128)(2,1)S(1)}, bf16[2,384,512]{2,1,0:T(8,128)(2,1)S(1)}, u32[]{:S(2)}, u32[]{:S(2)}) collective-permute-start(bf16[2,384,512]{2,1,0:T(8,128)(2,1)S(1)} %copy-done.34), channel_id=1, source_target_pairs={{0,8},{8,16},{16,24},{24,0},{1,9},{9,17},{17,25},{25,1},{2,10},{10... | collective-permute-start | bytes 2359304 | tf_op jit(solution)/shard_map/ppermute | solution.py:15
  63.0 78.5 %collective-permute-start.24 = (bf16[2,384,512]{2,1,0:T(8,128)(2,1)S(1)}, bf16[2,384,512]{2,1,0:T(8,128)(2,1)S(1)}, u32[]{:S(2)}, u32[]{:S(2)}) collective-permute-start(bf16[2,384,512]{2,1,0:T(8,128)(2,1)S(1)} %copy-done.34), channel_id=1, source_target_pairs={{0,16},{8,24},{16,0},{24,8},{1,17},{9,25},{17,1},{25,9},{2,18},{10... | collective-permute-start | bytes 2359304 | tf_op jit(solution)/shard_map/ppermute | solution.py:15
  83.1 32.0 %collective-permute-start.23 = (bf16[2,384,512]{2,1,0:T(8,128)(2,1)S(1)}, bf16[2,384,512]{2,1,0:T(8,128)(2,1)S(1)}, u32[]{:S(2)}, u32[]{:S(2)}) collective-permute-start(bf16[2,384,512]{2,1,0:T(8,128)(2,1)S(1)} %copy-done.34), channel_id=1, source_target_pairs={{0,24},{8,0},{16,8},{24,16},{1,25},{9,1},{17,9},{25,17},{2,26},{10... | collective-permute-start | bytes 2359304 | tf_op jit(solution)/shard_map/ppermute | solution.py:15
  89.7 52.7 %collective-permute-start.13 = (bf16[272,1536]{1,0:T(8,128)(2,1)}, bf16[272,1536]{1,0:T(8,128)(2,1)S(1)}, u32[]{:S(2)}, u32[]{:S(2)}) collective-permute-start(bf16[272,1536]{1,0:T(8,128)(2,1)} %collective-permute-done.12), channel_id=1, source_target_pairs={{0,1},{1,0},{2,3},{3,2},{4,5},{5,4},{6,7},{7,6},{8,9},{9,8},{10,11... | collective-permute-start | bytes 2506760 | tf_op jit(solution)/shard_map/ppermute | solution.py:34
  98.5 204.6 %collective-permute-start.36 = (bf16[272,1536]{1,0:T(8,128)(2,1)}, bf16[272,1536]{1,0:T(8,128)(2,1)}, u32[]{:S(2)}, u32[]{:S(2)}) collective-permute-start(bf16[272,1536]{1,0:T(8,128)(2,1)} %fusion.60), channel_id=1, source_target_pairs={{0,1},{1,0},{2,3},{3,2},{4,5},{5,4},{6,7},{7,6},{8,9},{9,8},{10,11... | collective-permute-start | bytes 2506760 | tf_op jit(solution)/shard_map/ppermute | solution.py:34
  100.6 64.8 %collective-permute-start.10 = (bf16[3,1152,192]{1,2,0:T(8,128)(2,1)S(1)}, bf16[3,1152,192]{1,2,0:T(8,128)(2,1)S(1)}, u32[]{:S(2)}, u32[]{:S(2)}) collective-permute-start(bf16[3,1152,192]{1,2,0:T(8,128)(2,1)S(1)} %pad_maximum_fusion.24), channel_id=1, source_target_pairs={{0,4},{2,6},{4,0},{6,2},{1,5},{3,7},{5,1},{7,3},{8,12},{10,14},{12... | collective-permute-start | bytes 3981320 | tf_op jit(solution)/shard_map/ppermute | solution.py:24
  115.1 32.0 %collective-permute-start.31 = (bf16[512,384]{1,0:T(8,128)(2,1)S(1)}, bf16[512,384]{1,0:T(8,128)(2,1)S(1)}, u32[]{:S(2)}, u32[]{:S(2)}) collective-permute-start(bf16[512,384]{1,0:T(8,128)(2,1)S(1)} %copy-done.46), channel_id=1, source_target_pairs={{0,8},{8,16},{16,24},{24,0},{1,9},{9,17},{17,25},{25,1},{2,10},{10... | collective-permute-start | bytes 1179656 | tf_op jit(solution)/shard_map/ppermute | solution.py:15
  147.1 46.3 %collective-permute-start.9 = (bf16[3,1536,192]{1,2,0:T(8,128)(2,1)S(1)}, bf16[3,1536,192]{1,2,0:T(8,128)(2,1)S(1)}, u32[]{:S(2)}, u32[]{:S(2)}) collective-permute-start(bf16[3,1536,192]{1,2,0:T(8,128)(2,1)S(1)} %pad_maximum_fusion.13), channel_id=1, source_target_pairs={{0,2},{2,0},{4,6},{6,4},{1,3},{3,1},{5,7},{7,5},{8,10},{10,8},{12,... | collective-permute-start | bytes 5308424 | tf_op jit(solution)/shard_map/ppermute | solution.py:28
  161.6 31.3 %collective-permute-start.14 = (bf16[544,1536]{1,0:T(8,128)(2,1)S(1)}, bf16[544,1536]{1,0:T(8,128)(2,1)S(1)}, u32[]{:S(2)}, u32[]{:S(2)}) collective-permute-start(bf16[544,1536]{1,0:T(8,128)(2,1)S(1)} %maximum_select_fusion), channel_id=1, source_target_pairs={{0,2},{2,0},{4,6},{6,4},{1,3},{3,1},{5,7},{7,5},{8,10},{10,8},{12,... | collective-permute-start | bytes 5013512 | tf_op jit(solution)/shard_map/ppermute | solution.py:28
  163.2 23.8 %collective-permute-start.33 = (bf16[512,1152]{1,0:T(8,128)(2,1)S(1)}, bf16[512,1152]{1,0:T(8,128)(2,1)S(1)}, u32[]{:S(2)}, u32[]{:S(2)}) collective-permute-start(bf16[512,1152]{1,0:T(8,128)(2,1)S(1)} %pad_maximum_fusion.25), channel_id=1, source_target_pairs={{0,4},{2,6},{4,0},{6,2},{1,5},{3,7},{5,1},{7,3},{8,12},{10,14},{12... | collective-permute-start | bytes 3538952 | tf_op jit(solution)/shard_map/ppermute | solution.py:24
  165.6 29.1 %collective-permute-start.11 = (bf16[3,1536,192]{1,2,0:T(8,128)(2,1)S(1)}, bf16[3,1536,192]{1,2,0:T(8,128)(2,1)S(1)}, u32[]{:S(2)}, u32[]{:S(2)}) collective-permute-start(bf16[3,1536,192]{1,2,0:T(8,128)(2,1)S(1)} %pad_maximum_fusion.14), channel_id=1, source_target_pairs={{0,2},{2,0},{4,6},{6,4},{1,3},{3,1},{5,7},{7,5},{8,10},{10,8},{12,... | collective-permute-start | bytes 5308424 | tf_op jit(solution)/shard_map/ppermute | solution.py:28
  187.0 110.4 %collective-permute-start.18 = (bf16[192,1536]{1,0:T(8,128)(2,1)}, bf16[192,1536]{1,0:T(8,128)(2,1)}, u32[]{:S(2)}, u32[]{:S(2)}) collective-permute-start(bf16[192,1536]{1,0:T(8,128)(2,1)} %constant_dynamic-update-slice_fusion.5), channel_id=1, source_target_pairs={{0,2},{2,0},{4,6},{6,4},{1,3},{3,1},{5,7},{7,5},{8,10},{10,8},{12,... | collective-permute-start | bytes 1769480 | tf_op jit(solution)/shard_map/ppermute | solution.py:28
  192.9 104.8 %collective-permute-start.20 = (bf16[192,1536]{1,0:T(8,128)(2,1)}, bf16[192,1536]{1,0:T(8,128)(2,1)}, u32[]{:S(2)}, u32[]{:S(2)}) collective-permute-start(bf16[192,1536]{1,0:T(8,128)(2,1)} %pad_maximum_fusion.34), channel_id=1, source_target_pairs={{0,2},{2,0},{4,6},{6,4},{1,3},{3,1},{5,7},{7,5},{8,10},{10,8},{12,... | collective-permute-start | bytes 1769480 | tf_op jit(solution)/shard_map/ppermute | solution.py:28
  193.4 108.3 %collective-permute-start.27 = (bf16[2,1152,512]{2,1,0:T(8,128)(2,1)}, bf16[2,1152,512]{2,1,0:T(8,128)(2,1)S(1)}, u32[]{:S(2)}, u32[]{:S(2)}) collective-permute-start(bf16[2,1152,512]{2,1,0:T(8,128)(2,1)} %pad_maximum_fusion.11), channel_id=1, source_target_pairs={{0,4},{2,6},{4,0},{6,2},{1,5},{3,7},{5,1},{7,3},{8,12},{10,14},{12... | collective-permute-start | bytes 7077896 | tf_op jit(solution)/shard_map/ppermute | solution.py:24
  194.6 147.2 %collective-permute-start.26 = (bf16[2,1536,512]{2,1,0:T(8,128)(2,1)}, bf16[2,1536,512]{2,1,0:T(8,128)(2,1)}, u32[]{:S(2)}, u32[]{:S(2)}) collective-permute-start(bf16[2,1536,512]{2,1,0:T(8,128)(2,1)} %constant_dynamic-update-slice_fusion.9), channel_id=1, source_target_pairs={{0,2},{2,0},{4,6},{6,4},{1,3},{3,1},{5,7},{7,5},{8,10},{10,8},{12,... | collective-permute-start | bytes 9437192 | tf_op jit(solution)/shard_map/ppermute | solution.py:28
  297.4 26.1 %collective-permute-start.32 = (bf16[512,1536]{1,0:T(8,128)(2,1)}, bf16[512,1536]{1,0:T(8,128)(2,1)}, u32[]{:S(2)}, u32[]{:S(2)}) collective-permute-start(bf16[512,1536]{1,0:T(8,128)(2,1)} %copy-done.75), channel_id=1, source_target_pairs={{0,2},{2,0},{4,6},{6,4},{1,3},{3,1},{5,7},{7,5},{8,10},{10,8},{12,... | collective-permute-start | bytes 4718600 | tf_op jit(solution)/shard_map/ppermute | solution.py:28
  297.7 25.7 %collective-permute-start.34 = (bf16[512,1536]{1,0:T(8,128)(2,1)}, bf16[512,1536]{1,0:T(8,128)(2,1)}, u32[]{:S(2)}, u32[]{:S(2)}) collective-permute-start(bf16[512,1536]{1,0:T(8,128)(2,1)} %pad_maximum_fusion.21), channel_id=1, source_target_pairs={{0,2},{2,0},{4,6},{6,4},{1,3},{3,1},{5,7},{7,5},{8,10},{10,8},{12,... | collective-permute-start | bytes 4718600 | tf_op jit(solution)/shard_map/ppermute | solution.py:28
  303.1 38.7 %collective-permute-start.28 = (bf16[2,1536,512]{2,1,0:T(8,128)(2,1)S(1)}, bf16[2,1536,512]{2,1,0:T(8,128)(2,1)S(1)}, u32[]{:S(2)}, u32[]{:S(2)}) collective-permute-start(bf16[2,1536,512]{2,1,0:T(8,128)(2,1)S(1)} %pad_maximum_fusion.7), channel_id=1, source_target_pairs={{0,2},{2,0},{4,6},{6,4},{1,3},{3,1},{5,7},{7,5},{8,10},{10,8},{12,... | collective-permute-start | bytes 9437192 | tf_op jit(solution)/shard_map/ppermute | solution.py:28
  409.8 39.1 %collective-permute-start.35 = (bf16[272,1536]{1,0:T(8,128)(2,1)S(1)}, bf16[272,1536]{1,0:T(8,128)(2,1)S(1)}, u32[]{:S(2)}, u32[]{:S(2)}) collective-permute-start(bf16[272,1536]{1,0:T(8,128)(2,1)S(1)} %dynamic-slice_convert_fusion.3), channel_id=1, source_target_pairs={{0,1},{1,0},{2,3},{3,2},{4,5},{5,4},{6,7},{7,6},{8,9},{9,8},{10,11... | collective-permute-start | bytes 2506760 | tf_op jit(solution)/shard_map/ppermute | solution.py:51
  435.1 155.3 %collective-permute-start.67 = (bf16[2,512,1536]{2,1,0:T(8,128)(2,1)}, bf16[2,512,1536]{2,1,0:T(8,128)(2,1)}, u32[]{:S(2)}, u32[]{:S(2)}) collective-permute-start(bf16[2,512,1536]{2,1,0:T(8,128)(2,1)} %pad_maximum_fusion.8), channel_id=1, source_target_pairs={{0,2},{2,0},{4,6},{6,4},{1,3},{3,1},{5,7},{7,5},{8,10},{10,8},{12,... | collective-permute-start | bytes 9437192 | tf_op jit(solution)/shard_map/ppermute | solution.py:28
  456.0 193.8 %collective-permute-start.59 = (bf16[2,2,1536,512]{3,2,1,0:T(8,128)(2,1)}, bf16[2,2,1536,512]{3,2,1,0:T(8,128)(2,1)}, u32[]{:S(2)}, u32[]{:S(2)}) collective-permute-start(bf16[2,2,1536,512]{3,2,1,0:T(8,128)(2,1)} %pad_maximum_fusion.4), channel_id=1, source_target_pairs={{0,2},{2,0},{4,6},{6,4},{1,3},{3,1},{5,7},{7,5},{8,10},{10,8},{12,... | collective-permute-start | bytes 18874376 | tf_op jit(solution)/shard_map/ppermute | solution.py:28
  548.2 39.6 %collective-permute-start.51 = (bf16[2,192,1536]{2,1,0:T(8,128)(2,1)}, bf16[2,192,1536]{2,1,0:T(8,128)(2,1)}, u32[]{:S(2)}, u32[]{:S(2)}) collective-permute-start(bf16[2,192,1536]{2,1,0:T(8,128)(2,1)} %pad_maximum_fusion.26), channel_id=1, source_target_pairs={{0,2},{2,0},{4,6},{6,4},{1,3},{3,1},{5,7},{7,5},{8,10},{10,8},{12,... | collective-permute-start | bytes 3538952 | tf_op jit(solution)/shard_map/ppermute | solution.py:28
  587.3 68.5 %collective-permute-start.43 = (bf16[2,3,1536,192]{2,3,1,0:T(8,128)(2,1)S(1)}, bf16[2,3,1536,192]{2,3,1,0:T(8,128)(2,1)S(1)}, u32[]{:S(2)}, u32[]{:S(2)}) collective-permute-start(bf16[2,3,1536,192]{2,3,1,0:T(8,128)(2,1)S(1)} %pad_maximum_fusion.5), channel_id=1, source_target_pairs={{0,2},{2,0},{4,6},{6,4},{1,3},{3,1},{5,7},{7,5},{8,10},{10,8},{12,... | collective-permute-start | bytes 10616840 | tf_op jit(solution)/shard_map/ppermute | solution.py:28
  624.2 24.0 %collective-permute-start.41 = (bf16[272,1536]{1,0:T(8,128)(2,1)}, bf16[272,1536]{1,0:T(8,128)(2,1)S(1)}, u32[]{:S(2)}, u32[]{:S(2)}) collective-permute-start(bf16[272,1536]{1,0:T(8,128)(2,1)} %dynamic-slice_convert_fusion), channel_id=1, source_target_pairs={{0,1},{1,0},{2,3},{3,2},{4,5},{5,4},{6,7},{7,6},{8,9},{9,8},{10,11... | collective-permute-start | bytes 2506760 | tf_op jit(solution)/shard_map/ppermute | solution.py:51
  644.4 35.6 %collective-permute-start.68 = (bf16[512,1536]{1,0:T(8,128)(2,1)S(1)}, bf16[512,1536]{1,0:T(8,128)(2,1)S(1)}, u32[]{:S(2)}, u32[]{:S(2)}) collective-permute-start(bf16[512,1536]{1,0:T(8,128)(2,1)S(1)} %copy-done.47), channel_id=1, source_target_pairs={{0,4},{2,6},{4,0},{6,2},{1,5},{3,7},{5,1},{7,3},{8,12},{10,14},{12... | collective-permute-start | bytes 4718600 | tf_op jit(solution)/shard_map/ppermute | solution.py:24
  645.0 38.7 %collective-permute-start.40 = (bf16[272,1536]{1,0:T(8,128)(2,1)S(1)}, bf16[272,1536]{1,0:T(8,128)(2,1)S(1)}, u32[]{:S(2)}, u32[]{:S(2)}) collective-permute-start(bf16[272,1536]{1,0:T(8,128)(2,1)S(1)} %dynamic-slice_convert_fusion.1), channel_id=1, source_target_pairs={{0,1},{1,0},{2,3},{3,2},{4,5},{5,4},{6,7},{7,6},{8,9},{9,8},{10,11... | collective-permute-start | bytes 2506760 | tf_op jit(solution)/shard_map/ppermute | solution.py:51
  648.5 49.6 %collective-permute-start.42 = (bf16[272,1536]{1,0:T(8,128)(2,1)S(1)}, bf16[272,1536]{1,0:T(8,128)(2,1)S(1)}, u32[]{:S(2)}, u32[]{:S(2)}) collective-permute-start(bf16[272,1536]{1,0:T(8,128)(2,1)S(1)} %add_convert_fusion.4), channel_id=1, source_target_pairs={{4,0},{6,2},{5,1},{7,3},{12,8},{14,10},{13,9},{15,11},{20,16},{22,... | collective-permute-start | bytes 2506760 | tf_op jit(solution)/shard_map/ppermute | solution.py:154
  653.6 212.9 %collective-permute-start.60 = (bf16[2,1536,512]{2,1,0:T(8,128)(2,1)}, bf16[2,1536,512]{2,1,0:T(8,128)(2,1)}, u32[]{:S(2)}, u32[]{:S(2)}) collective-permute-start(bf16[2,1536,512]{2,1,0:T(8,128)(2,1)} %fusion.12), channel_id=1, source_target_pairs={{0,4},{2,6},{4,0},{6,2},{1,5},{3,7},{5,1},{7,3},{8,12},{10,14},{12... | collective-permute-start | bytes 9437192 | tf_op jit(solution)/shard_map/ppermute | solution.py:24
  657.8 201.7 %collective-permute-start.44 = (bf16[3,1536,192]{1,2,0:T(8,128)(2,1)}, bf16[3,1536,192]{1,2,0:T(8,128)(2,1)}, u32[]{:S(2)}, u32[]{:S(2)}) collective-permute-start(bf16[3,1536,192]{1,2,0:T(8,128)(2,1)} %fusion.21), channel_id=1, source_target_pairs={{0,4},{2,6},{4,0},{6,2},{1,5},{3,7},{5,1},{7,3},{8,12},{10,14},{12... | collective-permute-start | bytes 5308424 | tf_op jit(solution)/shard_map/ppermute | solution.py:24
  683.7 174.0 %collective-permute-start.69 = (bf16[512,384]{1,0:T(8,128)(2,1)}, bf16[512,384]{1,0:T(8,128)(2,1)}, u32[]{:S(2)}, u32[]{:S(2)}) collective-permute-start(bf16[512,384]{1,0:T(8,128)(2,1)} %get-tuple-element.126), channel_id=1, source_target_pairs={{0,8},{8,16},{16,24},{24,0},{1,9},{9,17},{17,25},{25,1},{2,10},{10... | collective-permute-start | bytes 1179656 | tf_op jit(solution)/shard_map/ppermute | solution.py:20
  683.7 174.0 %collective-permute-start.71 = (bf16[512,384]{1,0:T(8,128)(2,1)}, bf16[512,384]{1,0:T(8,128)(2,1)}, u32[]{:S(2)}, u32[]{:S(2)}) collective-permute-start(bf16[512,384]{1,0:T(8,128)(2,1)} %get-tuple-element.127), channel_id=1, source_target_pairs={{0,24},{8,0},{16,8},{24,16},{1,25},{9,1},{17,9},{25,17},{2,26},{10... | collective-permute-start | bytes 1179656 | tf_op jit(solution)/shard_map/ppermute | solution.py:20
  698.0 159.6 %collective-permute-start.70 = (bf16[512,384]{1,0:T(8,128)(2,1)S(1)}, bf16[512,384]{1,0:T(8,128)(2,1)}, u32[]{:S(2)}, u32[]{:S(2)}) collective-permute-start(bf16[512,384]{1,0:T(8,128)(2,1)S(1)} %get-tuple-element.128), channel_id=1, source_target_pairs={{0,16},{8,24},{16,0},{24,8},{1,17},{9,25},{17,1},{25,9},{2,18},{10... | collective-permute-start | bytes 1179656 | tf_op jit(solution)/shard_map/ppermute | solution.py:20
  863.1 26.1 %collective-permute-start.47 = (bf16[3,384,192]{1,2,0:T(8,128)(2,1)S(1)}, bf16[3,384,192]{1,2,0:T(8,128)(2,1)S(1)}, u32[]{:S(2)}, u32[]{:S(2)}) collective-permute-start(bf16[3,384,192]{1,2,0:T(8,128)(2,1)S(1)} %get-tuple-element.109), channel_id=1, source_target_pairs={{0,24},{8,0},{16,8},{24,16},{1,25},{9,1},{17,9},{25,17},{2,26},{10... | collective-permute-start | bytes 1327112 | tf_op jit(solution)/shard_map/ppermute | solution.py:20
  866.5 52.5 %collective-permute-start.46 = (bf16[3,384,192]{1,2,0:T(8,128)(2,1)S(1)}, bf16[3,384,192]{1,2,0:T(8,128)(2,1)S(1)}, u32[]{:S(2)}, u32[]{:S(2)}) collective-permute-start(bf16[3,384,192]{1,2,0:T(8,128)(2,1)S(1)} %get-tuple-element.110), channel_id=1, source_target_pairs={{0,16},{8,24},{16,0},{24,8},{1,17},{9,25},{17,1},{25,9},{2,18},{10... | collective-permute-start | bytes 1327112 | tf_op jit(solution)/shard_map/ppermute | solution.py:20
  870.9 48.3 %collective-permute-start.61 = (bf16[2,384,512]{2,1,0:T(8,128)(2,1)S(1)}, bf16[2,384,512]{2,1,0:T(8,128)(2,1)S(1)}, u32[]{:S(2)}, u32[]{:S(2)}) collective-permute-start(bf16[2,384,512]{2,1,0:T(8,128)(2,1)S(1)} %get-tuple-element.93), channel_id=1, source_target_pairs={{0,8},{8,16},{16,24},{24,0},{1,9},{9,17},{17,25},{25,1},{2,10},{10... | collective-permute-start | bytes 2359304 | tf_op jit(solution)/shard_map/ppermute | solution.py:20
  871.3 55.1 %collective-permute-start.63 = (bf16[2,384,512]{2,1,0:T(8,128)(2,1)S(1)}, bf16[2,384,512]{2,1,0:T(8,128)(2,1)S(1)}, u32[]{:S(2)}, u32[]{:S(2)}) collective-permute-start(bf16[2,384,512]{2,1,0:T(8,128)(2,1)S(1)} %get-tuple-element.94), channel_id=1, source_target_pairs={{0,24},{8,0},{16,8},{24,16},{1,25},{9,1},{17,9},{25,17},{2,26},{10... | collective-permute-start | bytes 2359304 | tf_op jit(solution)/shard_map/ppermute | solution.py:20
  874.3 94.1 %collective-permute-start.62 = (bf16[2,384,512]{2,1,0:T(8,128)(2,1)S(1)}, bf16[2,384,512]{2,1,0:T(8,128)(2,1)S(1)}, u32[]{:S(2)}, u32[]{:S(2)}) collective-permute-start(bf16[2,384,512]{2,1,0:T(8,128)(2,1)S(1)} %get-tuple-element.95), channel_id=1, source_target_pairs={{0,16},{8,24},{16,0},{24,8},{1,17},{9,25},{17,1},{25,9},{2,18},{10... | collective-permute-start | bytes 2359304 | tf_op jit(solution)/shard_map/ppermute | solution.py:20
  889.2 82.5 %collective-permute-start.74 = (bf16[512,384]{1,0:T(8,128)(2,1)S(1)}, bf16[512,384]{1,0:T(8,128)(2,1)S(1)}, u32[]{:S(2)}, u32[]{:S(2)}) collective-permute-start(bf16[512,384]{1,0:T(8,128)(2,1)S(1)} %add_convert_fusion.10), channel_id=1, source_target_pairs={{0,2},{2,0},{4,6},{6,4},{1,3},{3,1},{5,7},{7,5},{8,10},{10,8},{12,... | collective-permute-start | bytes 1179656 | tf_op jit(solution)/shard_map/ppermute | solution.py:28
  919.0 52.7 %collective-permute-start.73 = (bf16[512,384]{1,0:T(8,128)(2,1)S(1)}, bf16[512,384]{1,0:T(8,128)(2,1)S(1)}, u32[]{:S(2)}, u32[]{:S(2)}) collective-permute-start(bf16[512,384]{1,0:T(8,128)(2,1)S(1)} %collective-permute-done.72), channel_id=1, source_target_pairs={{0,2},{2,0},{4,6},{6,4},{1,3},{3,1},{5,7},{7,5},{8,10},{10,8},{12,... | collective-permute-start | bytes 1179656 | tf_op jit(solution)/shard_map/ppermute | solution.py:28
  919.2 52.0 %collective-permute-start.48 = (bf16[3,384,192]{1,2,0:T(8,128)(2,1)S(1)}, bf16[3,384,192]{1,2,0:T(8,128)(2,1)S(1)}, u32[]{:S(2)}, u32[]{:S(2)}) collective-permute-start(bf16[3,384,192]{1,2,0:T(8,128)(2,1)S(1)} %add_convert_fusion.9), channel_id=1, source_target_pairs={{0,4},{2,6},{4,0},{6,2},{1,5},{3,7},{5,1},{7,3},{8,12},{10,14},{12... | collective-permute-start | bytes 1327112 | tf_op jit(solution)/shard_map/ppermute | solution.py:24
  (123 other events, 2966.7 us)
